TPU v7x, 32 devices: a whole 2x2x4 slice. The times are simulated.
32 devices in a mesh: dp: 16 (over z, y, x), tensor: 2 (over core).
Axes of the slice: x: 2, y: 2, z: 4, core: 2. Of those that a mesh axis runs over, the one named last changes fastest.
Arguments:
- tokens_in: bfloat16 [16384, 768], P('dp'), may hold values from -6 to 6
- cotangent: bfloat16 [16384, 768], P('dp'), may hold values from -6 to 6
- seq_lengths: int32 [16, 4], P('dp'), may hold values from 1 to 512, 1024 in all within a row
- q_weight: bfloat16 [768, 768], P(None, 'tensor'), may hold values from -0.4375 to 0.4375
- k_weight: bfloat16 [768, 768], P(None, 'tensor'), may hold values from -0.21875 to 0.21875
- v_weight: bfloat16 [768, 768], P(None, 'tensor'), may hold values from -0.21875 to 0.21875
- q_bias: float32 [768], P('tensor'), may hold values from -3 to 3
- v_bias: float32 [768], P('tensor'), may hold values from -3 to 3
- out_weight: bfloat16 [768, 768], P('tensor'), may hold values from -1 to 1
- out_bias: float32 [768], replicated, may hold values from -3 to 3
- first_gain: float32 [768], replicated, may hold values from 0.5 to 1.5
- first_shift: float32 [768], replicated, may hold values from -2 to 2
- up_weight: bfloat16 [768, 3072], P(None, 'tensor'), may hold values from -0.21875 to 0.21875
- up_bias: float32 [3072], P('tensor'), may hold values from -3 to 3
- down_weight: bfloat16 [3072, 768], P('tensor'), may hold values from -0.15625 to 0.15625
- down_bias: float32 [768], replicated, may hold values from -3 to 3
- second_gain: float32 [768], replicated, may hold values from 0.5 to 1.5
- second_shift: float32 [768], replicated, may hold values from -2 to 2
Outputs:
- layer_out: bfloat16 [16384, 768], P('dp')
- grad_input: bfloat16 [16384, 768], P('dp')
- grad_q_weight: float32 [768, 768], P(None, 'tensor')
- grad_k_weight: float32 [768, 768], P(None, 'tensor')
- grad_v_weight: float32 [768, 768], P(None, 'tensor')
- grad_q_bias: float32 [768], P('tensor')
- grad_v_bias: float32 [768], P('tensor')
- grad_out_weight: float32 [768, 768], P('tensor')
- grad_out_bias: float32 [768], replicated
- grad_first_gain: float32 [768], replicated
- grad_first_shift: float32 [768], replicated
- grad_up_weight: float32 [768, 3072], P(None, 'tensor')
- grad_up_bias: float32 [3072], P('tensor')
- grad_down_weight: float32 [3072, 768], P('tensor')
- grad_down_bias: float32 [768], replicated
- grad_second_gain: float32 [768], replicated
- grad_second_shift: float32 [768], replicated
Inputs may be any that keep to these rules, and one draw needn't show every extreme that they name: Each row of seq_lengths sums to 1024; in every row the longest sequence has exactly 512 tokens.
All inputs are finite; a program needn't handle non-finite values.
Results may differ from a plain program's by a relative error of at most 0.014.
The roundings to bfloat16 on the way count: a program that leaves them out, or rounds other values in their place, can miss the bound.
Values sent between devices are 32-bit elements; how exact they have to be, the bound alone decides.
No kernel may reach another device: no remote copies, remote signals or barrier semaphores. Data moves between devices by JAX's collectives and lax.ppermute only.
A program may use at most 192 MiB of HBM per device.

v0:
```python
import functools

import jax
import jax.numpy as jnp
from jax import lax
from jax.experimental import pallas as pl
from jax.experimental.pallas import tpu as pltpu
from jax.sharding import PartitionSpec as P

DH = 64
LANES = 128
QUERY_BLOCK = 256
ROW_BLOCK = 256
MIB = 1 << 20

score_scale = 0.125
norm_eps = 1e-05
far_negative = -1e30
log2_e = 1.4426950408889634


def contract(left_side, right_side, left_dim, right_dim):
    return lax.dot_general(
        left_side,
        right_side,
        (((left_dim,), (right_dim,)), ((), ())),
        preferred_element_type=jnp.float32,
    )


def sequence_ends(lengths_ref, count):
    ends = []
    total = jnp.int32(0)
    for at in range(count):
        total = total + lengths_ref[0, at]
        ends.append(total)
    return ends


def key_window(ends, first_row, rows):
    last_row = first_row + QUERY_BLOCK - 1
    start = jnp.int32(0)
    stop = jnp.int32(rows)
    for end in ends:
        start = jnp.where(end <= first_row, jnp.maximum(start, end), start)
        stop = jnp.where(end > last_row, jnp.minimum(stop, end), stop)
    start = (start // LANES) * LANES
    stop = ((stop + LANES - 1) // LANES) * LANES
    return start, stop


def window_bias(ends, first_row, key_start, width, key_axis):
    line = (1, QUERY_BLOCK) if key_axis == 0 else (QUERY_BLOCK, 1)
    whole = (width, QUERY_BLOCK) if key_axis == 0 else (QUERY_BLOCK, width)
    query_at = lax.broadcasted_iota(jnp.int32, line, 1 - key_axis) + first_row
    seq_start = jnp.zeros(line, jnp.int32)
    seq_stop = jnp.full(line, 1 << 30, jnp.int32)
    for end in ends:
        seq_start = jnp.where(query_at >= end, jnp.maximum(seq_start, end), seq_start)
        seq_stop = jnp.where(query_at < end, jnp.minimum(seq_stop, end), seq_stop)
    key_at = lax.broadcasted_iota(jnp.int32, whole, key_axis) + key_start
    seen = (key_at >= seq_start) & (key_at < seq_stop)
    bias = jnp.where(seen, 0.0, far_negative).astype(jnp.float32)
    return jnp.concatenate([bias, bias], axis=1 - key_axis)


def split_heads(block):
    lane = lax.broadcasted_iota(jnp.int32, block.shape, 1)
    wide = block.astype(jnp.float32)
    return jnp.concatenate(
        [jnp.where(lane < DH, wide, 0.0), jnp.where(lane < DH, 0.0, wide)], axis=0
    ).astype(jnp.bfloat16)


def merge_heads(stacked):
    rows = stacked.shape[0] // 2
    lane = lax.broadcasted_iota(jnp.int32, (rows, LANES), 1)
    return jnp.where(lane < DH, stacked[:rows], stacked[rows:]).astype(jnp.bfloat16)


def put_halves(moves, sent_far, kept_far, sums, mine):
    rows = sent_far.shape[0]
    for far, place in ((sent_far, 1 - mine), (kept_far, mine)):
        moves.out(sums.at[pl.ds(pl.multiple_of(place * rows, 8), rows), :], far)


def over_query_blocks(ends, rows, widths, body):
    @pl.loop(0, rows // QUERY_BLOCK)
    def _(block):
        first_row = pl.multiple_of(block * QUERY_BLOCK, QUERY_BLOCK)
        start, stop = key_window(ends, first_row, rows)
        span = stop - start
        lower = 0
        for width in widths:
            chosen = (span > lower) & (span <= width)
            key_start = pl.multiple_of(jnp.minimum(start, rows - width), LANES)
            pl.when(chosen)(functools.partial(body, block, first_row, key_start, width))
            lower = width


def row_mean(values):
    return jnp.mean(values, axis=-1, keepdims=True)


def standardize(values):
    centre = values - row_mean(values)
    rate = lax.rsqrt(row_mean(centre * centre) + norm_eps)
    return centre * rate, rate


def norm_back(upstream, unit, rate, gain):
    scaled = upstream * gain
    return rate * (scaled - row_mean(scaled) - unit * row_mean(scaled * unit))


def column_sum(member):
    return jnp.sum(member, axis=0, keepdims=True)


def row_blocks(rows):
    return [slice(at, at + ROW_BLOCK) for at in range(0, rows, ROW_BLOCK)]


class Moves:
    def __init__(self, semaphores):
        self.semaphores = semaphores
        self.used = 0
        self.outward = []

    def start(self, source, target):
        copy = pltpu.make_async_copy(source, target, self.semaphores.at[self.used])
        self.used += 1
        copy.start()
        return copy

    def out(self, source, target):
        self.outward.append(self.start(source, target))

    def finish(self):
        for copy in self.outward:
            copy.wait()


def attend_kernel(widths, seqs, *refs):
    (
        lengths_ref,
        tokens_far,
        q_weight_far,
        k_weight_far,
        v_weight_far,
        out_weight_far,
        q_bias_far,
        v_bias_far,
        queries_far,
        keys_far,
        values_far,
        context_far,
        totals_far,
        *parts_far,
        tokens_ref,
        q_weight_ref,
        k_weight_ref,
        v_weight_ref,
        out_weight_ref,
        queries_ref,
        keys_ref,
        values_ref,
        context_ref,
        total_ref,
        part_ref,
        q_bias_ref,
        v_bias_ref,
        semaphores,
    ) = refs
    rows = tokens_ref.shape[0]
    pairs = q_weight_ref.shape[1] // LANES
    moves = Moves(semaphores)
    tokens_in = moves.start(tokens_far, tokens_ref)
    biases_in = [moves.start(q_bias_far, q_bias_ref), moves.start(v_bias_far, v_bias_ref)]
    weights_in = [
        moves.start(far, near)
        for far, near in (
            (q_weight_far, q_weight_ref),
            (k_weight_far, k_weight_ref),
            (v_weight_far, v_weight_ref),
            (out_weight_far, out_weight_ref),
        )
    ]
    tokens_in.wait()
    for copy in biases_in:
        copy.wait()
    tokens = tokens_ref[...]
    for copy, weight_ref, bias, near, far in (
        (weights_in[0], q_weight_ref, q_bias_ref, queries_ref, queries_far),
        (weights_in[1], k_weight_ref, None, keys_ref, keys_far),
        (weights_in[2], v_weight_ref, v_bias_ref, values_ref, values_far),
    ):
        copy.wait()
        product = contract(tokens, weight_ref[...], 1, 0)
        if bias is not None:
            product = product + bias[...].reshape(1, -1)
        near[...] = product.astype(jnp.bfloat16)
        moves.out(near, far)
    ends = sequence_ends(lengths_ref, seqs)

    def body(block, first_row, key_start, width):
        bias = window_bias(ends, first_row, key_start, width, 1)
        for pair in range(pairs):
            lanes = slice(pair * LANES, (pair + 1) * LANES)
            both = split_heads(queries_ref[pl.ds(first_row, QUERY_BLOCK), lanes])
            keys = keys_ref[pl.ds(key_start, width), lanes]
            scores = contract(both, keys, 1, 1) * (score_scale * log2_e) + bias
            peak = jnp.max(scores, axis=1, keepdims=True)
            exponents = jnp.exp2(scores - peak)
            total = jnp.sum(exponents, axis=1, keepdims=True)
            spread = jnp.broadcast_to(peak + jnp.log2(total), (2 * QUERY_BLOCK, LANES))
            total_ref[pl.ds(block * pairs + pair, 1), :] = spread.T[0:1]
            probs = (exponents * (1.0 / total)).astype(jnp.bfloat16)
            context = contract(probs, values_ref[pl.ds(key_start, width), lanes], 1, 0)
            context_ref[pl.ds(first_row, QUERY_BLOCK), lanes] = merge_heads(context)

    over_query_blocks(ends, rows, widths, body)
    moves.out(context_ref, context_far)
    moves.out(total_ref, totals_far)
    weights_in[3].wait()
    for at, far in zip(row_blocks(rows), parts_far, strict=True):
        part_ref[at] = contract(context_ref[at], out_weight_ref[...], 1, 0)
        moves.out(part_ref.at[at], far)
    moves.finish()


def attend_back_kernel(widths, seqs, *refs):
    (
        lengths_ref,
        back_low_far,
        back_high_far,
        out_weight_far,
        queries_far,
        keys_far,
        values_far,
        totals_far,
        back_all_far,
        back_attn_ref,
        out_weight_ref,
        queries_ref,
        keys_ref,
        values_ref,
        total_ref,
        back_context_ref,
        back_all_ref,
        back_keys_ref,
        back_values_ref,
        semaphores,
    ) = refs
    rows, width_here = queries_ref.shape
    pairs = width_here // LANES
    half_rows = rows // 2
    moves = Moves(semaphores)
    early = [
        moves.start(far, near)
        for far, near in (
            (out_weight_far, out_weight_ref),
            (back_low_far, back_attn_ref.at[:half_rows]),
            (back_high_far, back_attn_ref.at[half_rows:]),
        )
    ]
    late = [
        moves.start(far, near)
        for far, near in (
            (queries_far, queries_ref),
            (keys_far, keys_ref),
            (values_far, values_ref),
            (totals_far, total_ref),
        )
    ]
    back_keys_ref[...] = jnp.zeros_like(back_keys_ref)
    back_values_ref[...] = jnp.zeros_like(back_values_ref)
    for copy in early:
        copy.wait()
    back_context_ref[...] = contract(back_attn_ref[...], out_weight_ref[...], 1, 1).astype(
        jnp.bfloat16
    )
    for copy in late:
        copy.wait()
    ends = sequence_ends(lengths_ref, seqs)

    def body(block, first_row, key_start, width):
        bias = window_bias(ends, first_row, key_start, width, 0)
        for pair in range(pairs):
            lanes = slice(pair * LANES, (pair + 1) * LANES)
            both = split_heads(queries_ref[pl.ds(first_row, QUERY_BLOCK), lanes])
            back_both = split_heads(back_context_ref[pl.ds(first_row, QUERY_BLOCK), lanes])
            keys = keys_ref[pl.ds(key_start, width), lanes]
            values = values_ref[pl.ds(key_start, width), lanes]
            scores = contract(keys, both, 1, 1) * (score_scale * log2_e) + bias
            probs = jnp.exp2(scores - total_ref[pl.ds(block * pairs + pair, 1), :])
            back_probs = contract(values, back_both, 1, 1)
            inner = jnp.sum(back_probs * probs, axis=0, keepdims=True)
            back_scores = (probs * (back_probs - inner) * score_scale).astype(jnp.bfloat16)
            back_values_ref[pl.ds(key_start, width), lanes] += contract(
                probs.astype(jnp.bfloat16), back_both, 1, 0
            )
            back_keys_ref[pl.ds(key_start, width), lanes] += contract(back_scores, both, 1, 0)
            back_queries = contract(back_scores, keys, 0, 0)
            back_all_ref[pl.ds(first_row, QUERY_BLOCK), lanes] = merge_heads(back_queries)

    over_query_blocks(ends, rows, widths, body)
    back_all_ref[:, width_here : 2 * width_here] = back_keys_ref[...].astype(jnp.bfloat16)
    back_all_ref[:, 2 * width_here :] = back_values_ref[...].astype(jnp.bfloat16)
    moves.out(back_all_ref, back_all_far)
    moves.finish()


def grad_attn_kernel(*refs):
    (
        bits_ref,
        tokens_far,
        back_all_far,
        context_far,
        back_low_far,
        back_high_far,
        small_ref,
        first_sent_far,
        first_kept_far,
        second_sent_far,
        second_kept_far,
        tokens_ref,
        back_all_ref,
        context_ref,
        back_attn_ref,
        first_pack_ref,
        second_pack_ref,
        semaphores,
    ) = refs
    rows, model = tokens_ref.shape
    width_here = context_ref.shape[1]
    half_rows = rows // 2
    moves = Moves(semaphores)
    arriving = [
        moves.start(far, near)
        for far, near in (
            (tokens_far, tokens_ref),
            (back_all_far, back_all_ref),
            (context_far, context_ref),
            (back_low_far, back_attn_ref.at[:half_rows]),
            (back_high_far, back_attn_ref.at[half_rows:]),
        )
    ]
    for copy in arriving[:2]:
        copy.wait()
    tokens = tokens_ref[...]
    first_pack_ref[...] = contract(tokens, back_all_ref[:, : 2 * width_here], 0, 0)
    put_halves(moves, first_sent_far, first_kept_far, first_pack_ref, bits_ref[0, 0])
    grad_values = contract(tokens, back_all_ref[:, 2 * width_here :], 0, 0)
    for copy in arriving[2:]:
        copy.wait()
    grad_out = contract(context_ref[...], back_attn_ref[...], 0, 0)
    out_half, value_half, small_half = width_here // 2, model // 4, small_ref.shape[0] // 2
    top = 0
    for at in range(2):
        second_pack_ref[top : top + out_half, :] = grad_out[at * out_half : (at + 1) * out_half]
        top += out_half
        for side in range(2):
            start = side * (model // 2) + at * value_half
            second_pack_ref[
                top : top + value_half, side * width_here : (side + 1) * width_here
            ] = grad_values[start : start + value_half]
        top += value_half
        second_pack_ref[top : top + small_half, :] = small_ref[
            at * small_half : (at + 1) * small_half
        ]
        if at == 0:
            for side in range(2):
                member = back_all_ref[:, 2 * side * width_here : (2 * side + 1) * width_here]
                second_pack_ref[top : top + 1, side * width_here : (side + 1) * width_here] = (
                    column_sum(member.astype(jnp.float32))
                )
        top += small_half
    put_halves(moves, second_sent_far, second_kept_far, second_pack_ref, bits_ref[0, 1])
    moves.finish()


def input_part_kernel(*refs):
    (
        back_all_far,
        q_weight_far,
        k_weight_far,
        v_weight_far,
        *parts_far,
        back_all_ref,
        weights_ref,
        part_ref,
        semaphores,
    ) = refs
    width_here = q_weight_far.shape[1]
    moves = Moves(semaphores)
    arriving = [
        moves.start(far, weights_ref.at[:, at * width_here : (at + 1) * width_here])
        for at, far in enumerate((q_weight_far, k_weight_far, v_weight_far))
    ]
    blocks = row_blocks(back_all_ref.shape[0])
    arriving += [moves.start(back_all_far.at[at], back_all_ref.at[at]) for at in blocks]
    for copy in arriving:
        copy.wait()
    for at, far in zip(blocks, parts_far, strict=True):
        part_ref[at] = contract(back_all_ref[at], weights_ref[...], 1, 1)
        moves.out(part_ref.at[at], far)
    moves.finish()


def feed_kernel(first_row, *refs):
    (
        tokens_far,
        *own_fars,
        out_bias_ref,
        gain_ref,
        shift_ref,
        up_weight_ref,
        up_bias_ref,
        down_weight_far,
        first_sum_far,
        first_low_far,
        active_far,
        part_low_far,
        part_high_far,
        tokens_ref,
        own_ref,
        first_sum_ref,
        first_low_ref,
        active_ref,
        part_ref,
        down_weight_ref,
        semaphores,
    ) = refs
    rows = own_ref.shape[0]
    own_fars, other_refs = own_fars[: len(own_fars) // 2], own_fars[len(own_fars) // 2 :]
    moves = Moves(semaphores)
    arriving = []
    for at, own_far in zip(row_blocks(rows), own_fars, strict=True):
        there = slice(first_row + at.start, first_row + at.stop)
        arriving.append(
            (
                moves.start(own_far, own_ref.at[at]),
                moves.start(tokens_far.at[there], tokens_ref.at[at]),
            )
        )
        if at.start == 0:
            down_in = moves.start(down_weight_far, down_weight_ref)
    for at, copies, other_ref, part_far in zip(
        row_blocks(rows), arriving, other_refs, (part_low_far, part_high_far), strict=True
    ):
        for copy in copies:
            copy.wait()
        first_sum = (
            tokens_ref[at].astype(jnp.float32)
            + (own_ref[at] + other_ref[...])
            + out_bias_ref[...].reshape(1, -1)
        )
        first_sum_ref[at] = first_sum
        moves.out(first_sum_ref.at[at], first_sum_far.at[at])
        unit, unused = standardize(first_sum)
        first_low = (
            unit * gain_ref[...].reshape(1, -1) + shift_ref[...].reshape(1, -1)
        ).astype(jnp.bfloat16)
        first_low_ref[at] = first_low
        moves.out(first_low_ref.at[at], first_low_far.at[at])
        inner = contract(first_low, up_weight_ref[...], 1, 0) + up_bias_ref[...].reshape(1, -1)
        active = (inner * (0.5 * (1.0 + lax.erf(inner * 0.7071067811865476)))).astype(
            jnp.bfloat16
        )
        active_ref[at] = active
        moves.out(active_ref.at[at], active_far.at[at])
        if at.start == 0:
            down_in.wait()
        part_ref[at] = contract(active, down_weight_ref[...], 1, 0)
        moves.out(part_ref.at[at], part_far)
    moves.finish()


def second_norm_kernel(first_row, last, *refs):
    refs = list(refs)
    if last:
        bits_ref, active_low_far, active_high_far, back_low_far, layer_before_far = refs[:5]
        del refs[:5]
    (
        first_sum_far,
        own_low_far,
        own_high_far,
        *other_refs,
        cotangent_far,
        first_gain_ref,
        first_shift_ref,
        down_bias_ref,
        gain_ref,
        shift_ref,
    ) = refs[:11]
    layer_far, back_second_far, back_down_far, sums_ref = refs[11:15]
    rest = refs[15:]
    if last:
        grads_far, rest = rest[:4], rest[4:]
    first_sum_ref, own_ref, cotangent_ref, layer_ref, back_second_ref, back_down_ref, *rest = rest
    semaphores = rest[-1]
    rows = own_ref.shape[0]
    moves = Moves(semaphores)
    arriving = []
    for at, own_far in zip(row_blocks(rows), (own_low_far, own_high_far), strict=True):
        there = slice(first_row + at.start, first_row + at.stop)
        arriving.append(
            (
                moves.start(own_far, own_ref.at[at]),
                moves.start(first_sum_far.at[at], first_sum_ref.at[at]),
                moves.start(cotangent_far.at[there], cotangent_ref.at[at]),
            )
        )
    if last:
        active_ref, back_before_ref, grads_ref, unused = rest
        early = [
            moves.start(active_low_far, active_ref.at[:rows]),
            moves.start(back_low_far, back_before_ref),
        ]
        late = moves.start(active_high_far, active_ref.at[rows:])
    bias_sum, gain_sum, shift_sum = 0.0, 0.0, 0.0
    gain = gain_ref[...].reshape(1, -1)
    shift = shift_ref[...].reshape(1, -1)
    for at, copies, other_ref in zip(row_blocks(rows), arriving, other_refs, strict=True):
        for copy in copies:
            copy.wait()
        unit, unused = standardize(first_sum_ref[at])
        first = unit * first_gain_ref[...].reshape(1, -1) + first_shift_ref[...].reshape(1, -1)
        second_sum = first + (own_ref[at] + other_ref[...]) + down_bias_ref[...].reshape(1, -1)
        unit, rate = standardize(second_sum)
        layer_ref[at] = (unit * gain + shift).astype(jnp.bfloat16)
        there = slice(first_row + at.start, first_row + at.stop)
        moves.out(layer_ref.at[at], layer_far.at[there])
        upstream = cotangent_ref[at].astype(jnp.float32)
        back_second = norm_back(upstream, unit, rate, gain)
        back_second_ref[at] = back_second
        moves.out(back_second_ref.at[at], back_second_far.at[at])
        back_down_ref[at] = back_second.astype(jnp.bfloat16)
        moves.out(back_down_ref.at[at], back_down_far.at[at])
        bias_sum += column_sum(back_second)
        gain_sum += column_sum(upstream * unit)
        shift_sum += column_sum(upstream)
    put_sums(sums_ref, bias_sum, gain_sum, shift_sum)
    if last:
        for copy in early:
            copy.wait()
        late.wait()
        height = grads_ref.shape[1]
        for slot, (block, same) in enumerate(((0, False), (1, False), (0, True), (1, True))):
            mine = bits_ref[0, block]
            place = mine if same else 1 - mine
            units = pl.ds(pl.multiple_of((2 * block + place) * height, LANES), height)
            grads_ref[slot] = contract(
                active_ref[:rows, units], back_before_ref[...], 0, 0
            ) + contract(active_ref[rows:, units], back_down_ref[...], 0, 0)
            moves.out(grads_ref.at[slot], grads_far[slot])
    moves.finish()


def put_sums(sums_ref, *members):
    sums_ref[...] = jnp.zeros_like(sums_ref)
    for at, member in enumerate(members):
        sums_ref[at : at + 1, :] = member


def feed_back_kernel(last, *refs):
    refs = list(refs)
    if last:
        bits_ref, first_before_far, inner_before_far = refs[:3]
        del refs[:3]
    (
        back_down_far,
        first_low_far,
        up_weight_ref,
        up_bias_ref,
        down_weight_ref,
        part_low_far,
        part_high_far,
        inner_far,
        sums_ref,
        *rest,
    ) = refs
    if last:
        grads_far, rest = rest[:4], rest[4:]
    back_down_ref, first_low_ref, part_ref, inner_ref, *rest = rest
    semaphores = rest[-1]
    rows = back_down_ref.shape[0]
    moves = Moves(semaphores)
    arriving = [
        (
            moves.start(first_low_far.at[at], first_low_ref.at[at]),
            moves.start(back_down_far.at[at], back_down_ref.at[at]),
        )
        for at in row_blocks(rows)
    ]
    if last:
        first_before_ref, inner_before_ref, grads_ref, unused = rest
        late = [
            moves.start(first_before_far, first_before_ref),
            moves.start(inner_before_far, inner_before_ref),
        ]
    total = 0.0
    for at, copies, part_far in zip(
        row_blocks(rows), arriving, (part_low_far, part_high_far), strict=True
    ):
        for copy in copies:
            copy.wait()
        inner = contract(first_low_ref[at], up_weight_ref[...], 1, 0) + up_bias_ref[...].reshape(
            1, -1
        )
        slope = 0.5 * (1.0 + lax.erf(inner * 0.7071067811865476)) + inner * (
            0.3989422804014327 * jnp.exp(-0.5 * inner * inner)
        )
        back_active = contract(back_down_ref[at], down_weight_ref[...], 1, 1)
        back_inner = (back_active * slope).astype(jnp.bfloat16)
        inner_ref[at] = back_inner
        if not last:
            moves.out(inner_ref.at[at], inner_far.at[at])
        part_ref[at] = contract(back_inner, up_weight_ref[...], 1, 1)
        moves.out(part_ref.at[at], part_far)
        total += column_sum(back_inner.astype(jnp.float32))
    put_sums(sums_ref, total)
    if last:
        moves.out(inner_ref.at[:16], inner_far)
        for copy in late:
            copy.wait()
        height, columns = grads_ref.shape[1:]
        for slot, (block, same) in enumerate(((0, False), (1, False), (0, True), (1, True))):
            mine = bits_ref[0, block]
            place = mine if same else 1 - mine
            features = pl.ds(pl.multiple_of(place * height, LANES), height)
            units = slice(block * columns, (block + 1) * columns)
            grads_ref[slot] = contract(
                first_before_ref[:, features], inner_before_ref[:, units], 0, 0
            ) + contract(first_low_ref[:, features], inner_ref[:, units], 0, 0)
            moves.out(grads_ref.at[slot], grads_far[slot])
    moves.finish()


def first_norm_kernel(*refs):
    (
        first_sum_far,
        own_low_far,
        own_high_far,
        *other_refs,
        back_second_far,
        gain_ref,
        back_first_far,
        back_attn_far,
        sums_ref,
        first_sum_ref,
        own_ref,
        back_second_ref,
        back_first_ref,
        back_attn_ref,
        semaphores,
    ) = refs
    rows = own_ref.shape[0]
    moves = Moves(semaphores)
    arriving = [
        (
            moves.start(own_far, own_ref.at[at]),
            moves.start(first_sum_far.at[at], first_sum_ref.at[at]),
            moves.start(back_second_far.at[at], back_second_ref.at[at]),
        )
        for at, own_far in zip(row_blocks(rows), (own_low_far, own_high_far), strict=True)
    ]
    bias_sum, gain_sum, shift_sum = 0.0, 0.0, 0.0
    gain = gain_ref[...].reshape(1, -1)
    for at, copies, other_ref in zip(row_blocks(rows), arriving, other_refs, strict=True):
        for copy in copies:
            copy.wait()
        unit, rate = standardize(first_sum_ref[at])
        upstream = (own_ref[at] + other_ref[...]) + back_second_ref[at]
        back_first_sum = norm_back(upstream, unit, rate, gain)
        back_first_ref[at] = back_first_sum
        moves.out(back_first_ref.at[at], back_first_far.at[at])
        back_attn_ref[at] = back_first_sum.astype(jnp.bfloat16)
        moves.out(back_attn_ref.at[at], back_attn_far.at[at])
        bias_sum += column_sum(back_first_sum)
        gain_sum += column_sum(upstream * unit)
        shift_sum += column_sum(upstream)
    put_sums(sums_ref, bias_sum, gain_sum, shift_sum)
    moves.finish()


def input_kernel(blocks, *refs):
    own_fars, other_refs = refs[:blocks], refs[blocks : 2 * blocks]
    *first_fars, grad_far, own_ref, first_ref, grad_ref, semaphores = refs[2 * blocks :]
    rows = own_ref.shape[0]
    moves = Moves(semaphores)
    arriving = []
    per = blocks // len(first_fars)
    for block, (at, own_far) in enumerate(zip(row_blocks(rows), own_fars, strict=True)):
        inside = slice(block % per * ROW_BLOCK, (block % per + 1) * ROW_BLOCK)
        arriving.append(
            (
                moves.start(own_far, own_ref.at[at]),
                moves.start(first_fars[block // per].at[inside], first_ref.at[at]),
            )
        )
    for at, copies, other_ref in zip(row_blocks(rows), arriving, other_refs, strict=True):
        for copy in copies:
            copy.wait()
        grad_ref[at] = ((own_ref[at] + other_ref[...]) + first_ref[at]).astype(jnp.bfloat16)
        moves.out(grad_ref.at[at], grad_far.at[at])
    moves.finish()


def struct(shape, dtype):
    return jax.ShapeDtypeStruct(shape, dtype)


def in_smem():
    return pl.BlockSpec(memory_space=pltpu.SMEM)


def in_vmem():
    return pl.BlockSpec(memory_space=pltpu.VMEM)


def in_hbm():
    return pl.BlockSpec(memory_space=pltpu.HBM)


def key_widths(rows):
    return tuple(width for width in (512, 768) if width < rows) + (rows,)


def call(body, name, operands, outs, scratch=(), near=(), near_outs=(), scalars=0, room=4, aliases=None):
    bytes_here = sum(
        jnp.dtype(dtype).itemsize * functools.reduce(lambda a, b: a * b, shape) for shape, dtype in scratch
    )
    specs = [
        in_smem() if at < scalars else in_vmem() if at in near else in_hbm()
        for at in range(len(operands))
    ]
    return pl.pallas_call(
        body,
        out_shape=tuple(
            struct(*out) if at in near_outs else pltpu.HBM(*out) for at, out in enumerate(outs)
        ),
        in_specs=specs,
        out_specs=tuple(in_vmem() if at in near_outs else in_hbm() for at in range(len(outs))),
        scratch_shapes=[pltpu.VMEM(*shape) for shape in scratch]
        + [pltpu.SemaphoreType.DMA((48,))],
        input_output_aliases=aliases or {},
        compiler_params=pltpu.CompilerParams(vmem_limit_bytes=bytes_here + room * MIB),
        name=name,
    )(
        *(
            operand
            if at < scalars or at in near
            else pltpu.with_memory_space_constraint(operand, pltpu.HBM)
            for at, operand in enumerate(operands)
        )
    )


low, exact = jnp.bfloat16, jnp.float32


def place_kernel(moves, starts_ref, *refs):
    copies = []
    inputs = 1 + max(source for source, *unused in moves)
    for at, (source, rows, columns, target, row_start, column_start) in enumerate(moves):
        start = row_start(starts_ref) if callable(row_start) else row_start
        size = rows[1] - rows[0]
        copies.append(
            pltpu.make_async_copy(
                refs[source].at[pl.ds(rows[0], size), pl.ds(columns[0], columns[1] - columns[0])],
                refs[inputs + target].at[
                    pl.ds(pl.multiple_of(start, 8), size),
                    pl.ds(column_start, columns[1] - columns[0]),
                ],
                refs[-1].at[at],
            )
        )
    for copy in copies:
        copy.start()
    for copy in copies:
        copy.wait()


def place_blocks(starts, operands, shapes, moves, name):
    anywhere = pl.BlockSpec(memory_space=pl.ANY)
    return pl.pallas_call(
        functools.partial(place_kernel, moves),
        out_shape=tuple(struct(shape, jnp.float32) for shape in shapes),
        in_specs=[in_smem()] + [in_vmem()] * len(operands),
        out_specs=(anywhere,) * len(shapes),
        scratch_shapes=[pltpu.SemaphoreType.DMA((len(moves),))],
        compiler_params=pltpu.CompilerParams(vmem_limit_bytes=4 * MIB),
        name=name,
    )(starts, *operands)


def at_bit(rows, bit, same):
    def first(bits_ref):
        return (bits_ref[0, bit] if same else 1 - bits_ref[0, bit]) * rows

    return first


def swap_cores(value, tensor_count):
    return lax.ppermute(value, "tensor", [(i, i ^ 1) for i in range(tensor_count)])


class Ring:
    def __init__(self, count, place):
        self.count = count
        self.place = place
        top = count.bit_length() - 1
        self.bits = (0, 1, top - 2, top - 1)
        self.between = range(2, top - 2)

    def swap(self, value, bit):
        return lax.ppermute(value, "dp", [(i, i ^ (1 << bit)) for i in range(self.count)])

    def mine(self, name):
        return (self.place >> self.bits[name]) & 1

    def half(self, value, name, same):
        rows = value.shape[0] // 2
        mine = self.mine(name)
        return lax.dynamic_slice_in_dim(value, (mine if same else 1 - mine) * rows, rows, 0)


class Chunk:
    def __init__(self, ring, bits, path, sent, kept):
        self.ring = ring
        self.bits = bits
        *self.path, self.middle = path
        self.held = (kept,)
        self.arriving = None
        self.sent = sent
        self.step = 0

    def inputs(self):
        return self.held + (() if self.arriving is None else (self.arriving,))

    def swap(self, value, name):
        self.arriving = self.ring.swap(value, self.ring.bits[name])

    def join(self, value, arriving, name):
        rows, columns = value.shape
        [joined] = place_blocks(
            self.bits,
            (value, arriving),
            ((2 * rows, columns),),
            (
                (0, (0, rows), (0, columns), 0, at_bit(rows, name, True), 0),
                (1, (0, rows), (0, columns), 0, at_bit(rows, name, False), 0),
            ),
            "join",
        )
        return joined

    def advance(self, inputs):
        ring = self.ring
        step = self.step
        depth = len(self.path)
        self.step += 1
        if step == 0:
            self.swap(self.sent, self.path[0])
            return None
        if step < depth:
            name = self.path[step]
            sent = functools.reduce(jnp.add, [ring.half(member, name, False) for member in inputs])
            self.held = tuple(ring.half(member, name, True) for member in inputs)
            self.swap(sent, name)
            return sent
        if step == depth:
            value = functools.reduce(jnp.add, inputs)
            for bit in ring.between:
                value = value + ring.swap(value, bit)
            self.swap(value, self.middle)
        else:
            value, arrived = inputs
            back = 2 * depth - step
            if back == depth - 1:
                value = value + arrived
            else:
                value = self.join(value, arrived, self.path[back + 1])
            self.swap(value, self.path[back])
        self.held = (value,)
        return value


class Sequence:
    def __init__(self):
        self.last = None

    def after(self, values):
        if self.last is None:
            return tuple(values)
        held = lax.optimization_barrier((*values, self.last))
        return held[:-1]

    def ran(self, result):
        if result is not None:
            self.last = result


paths = {
    "D0": (0, 1, 2, 3),
    "D1": (1, 2, 0, 3),
    "U0": (0, 1, 2, 3),
    "U1": (1, 2, 0, 3),
    "A0": (0, 1, 2, 3),
    "A1": (1, 0, 2, 3),
}

plan = (
    "D1", "D0", "FB0", "FB1", "LN", "D1", "D0", "LN", "AB", "U1", "D0", "U0", "D1", "U0", "GA",
    "A1", "D0", "U1", "A0", "U0", "U1", "D0", "D1", "U0", "D1", "U1", "A0", "A1", "D0", "D1", "U0",
    "A0", "U1", "D0", "D1", "A1", "U0", "U1", "A0", "A1", "U1", "A1", "U0", "PD", "A0", "A0", "A1",
    "IP", "PU", "A1", "A0", "GI", "PA",
)


def local(
    dp_count,
    tensor_count,
    tokens_in,
    cotangent,
    seq_lengths,
    q_weight,
    k_weight,
    v_weight,
    q_bias,
    v_bias,
    out_weight,
    out_bias,
    first_gain,
    first_shift,
    up_weight,
    up_bias,
    down_weight,
    down_bias,
    second_gain,
    second_shift,
):
    place = lax.axis_index("dp")
    ring = Ring(dp_count, place)
    bits = jnp.stack([ring.mine(name) for name in range(4)]).reshape(1, 4)

    def first_bits(name):
        return jnp.stack([ring.mine(paths[name + at][0]) for at in "01"]).reshape(1, 2)

    model = q_weight.shape[0]
    width = q_weight.shape[1]
    hidden = up_weight.shape[1]
    rows = tokens_in.shape[0]
    half_rows = rows // 2
    block = (ROW_BLOCK, model)
    blocks = rows // ROW_BLOCK
    half_blocks = blocks // 2
    half_exact = ((half_rows, model), exact)
    half_low = ((half_rows, model), low)
    half_active = ((half_rows, hidden), low)
    rows_width = ((rows, width), low)
    into = ((model, width), low)
    outof = ((width, model), low)
    seqs = seq_lengths.shape[1]
    widths = key_widths(rows)
    totals_shape = ((rows // QUERY_BLOCK * (width // LANES), 2 * QUERY_BLOCK), exact)
    queries, keys, values, context, totals, *attn_parts = call(
        functools.partial(attend_kernel, widths, seqs),
        "attend",
        (seq_lengths, tokens_in, q_weight, k_weight, v_weight, out_weight, q_bias, v_bias),
        [rows_width] * 4 + [totals_shape] + [(block, exact)] * blocks,
        [((rows, model), low), into, into, into, outof]
        + [rows_width] * 4
        + [totals_shape, ((rows, model), exact)]
        + [((width,), exact)] * 2,
        scalars=1,
        room=8,
    )
    order = Sequence()

    def swapped(parts):
        return tuple(swap_cores(part, tensor_count) for part in parts)

    attn_others = swapped(attn_parts)
    fed = []
    for at in range(2):
        mine = slice(at * half_blocks, (at + 1) * half_blocks)
        fed.append(
            call(
                functools.partial(feed_kernel, at * half_rows),
                "feed",
                (tokens_in, *attn_parts[mine], *attn_others[mine])
                + (out_bias, first_gain, first_shift, up_weight, up_bias, down_weight),
                [half_exact, half_low, half_active] + [(block, exact)] * half_blocks,
                [half_low, half_exact, half_exact, half_low, half_active, half_exact]
                + [((hidden, model), low)],
                near=range(1 + half_blocks, 1 + 2 * half_blocks + 5),
            )
        )
    first_sums, first_lows, actives = zip(*[member[:3] for member in fed], strict=True)
    down_parts = [member[3:] for member in fed]
    down_others = [swapped(parts) for parts in down_parts]
    second_vectors = (first_gain, first_shift, down_bias, second_gain, second_shift)
    sums_shape = ((8, model), exact)

    def second_norm(at, before, scratch, extra_outs):
        lead = len(before)
        return call(
            functools.partial(second_norm_kernel, at * half_rows, at == 1),
            "second_norm",
            (*before, first_sums[at], *down_parts[at], *down_others[at], cotangent)
            + second_vectors,
            [((rows, model), low), half_exact, half_low, sums_shape] + extra_outs,
            [half_exact, half_exact, half_low, half_low, half_exact, half_low] + scratch,
            near=[*range(lead + 1 + half_blocks, lead + 1 + 2 * half_blocks)]
            + [*range(lead + 2 + 2 * half_blocks, lead + 7 + 2 * half_blocks)],
            near_outs=(3,),
            scalars=1 if before else 0,
            room=8,
            aliases={4: 0} if before else None,
        )

    layer_out, back_second, back_down, second_sums = second_norm(0, (), [], [])
    down_piece = (hidden // 4, model)
    layer_out, *rest = second_norm(
        1,
        (first_bits("D"), *actives, back_down, layer_out),
        [((rows, hidden), low), half_low, ((4, *down_piece), exact)],
        [(down_piece, exact)] * 4,
    )
    back_seconds, back_downs = (back_second, rest[0]), (back_down, rest[1])
    second_sums = second_sums + rest[2]
    down_pieces = rest[3:]
    order.ran(down_pieces[0])
    chunks = {}

    def begin(name, pieces):
        chunks[name + "0"] = Chunk(ring, bits, paths[name + "0"], pieces[0], pieces[2])
        chunks[name + "1"] = Chunk(ring, bits, paths[name + "1"], pieces[1], pieces[3])

    def run(*names):
        for name in names:
            chunk = chunks[name]
            inputs = chunk.inputs()
            order.ran(chunk.advance(order.after(inputs) if chunk.step else inputs))

    up_piece = (model // 2, hidden // 2)
    fed_back = []
    normed_back = []
    made = {}

    def feed_back(at, before, inner_rows, scratch, extra_outs):
        [back_down] = order.after((back_downs[at],))
        lead = len(before)
        results = call(
            functools.partial(feed_back_kernel, at == 1),
            "feed_back",
            (*before, back_down, first_lows[at], up_weight, up_bias, down_weight),
            [(block, exact)] * half_blocks
            + [((inner_rows, hidden), low), ((8, hidden), exact)]
            + extra_outs,
            [half_low, half_low, half_exact, half_active] + scratch,
            near=range(lead + 2, lead + 5),
            near_outs=(half_blocks + 1,),
            scalars=1 if before else 0,
            room=6,
        )
        order.ran(results[half_blocks])
        fed_back.append(results)

    def feed_back_first():
        feed_back(0, (), half_rows, [], [])

    def feed_back_last():
        feed_back(
            1,
            (first_bits("U"), first_lows[0], fed_back[0][half_blocks]),
            16,
            [half_low, half_active, ((4, *up_piece), exact)],
            [(up_piece, exact)] * 4,
        )
        begin("U", fed_back[1][half_blocks + 2 :])

    def first_norm_back():
        at = len(normed_back)
        parts = fed_back[at][:half_blocks]
        others = order.after(swapped(parts))
        normed_back.append(
            call(
                first_norm_kernel,
                "first_norm_back",
                (first_sums[at], *parts, *others, back_seconds[at], first_gain),
                [half_exact, half_low, sums_shape],
                [half_exact, half_exact, half_exact, half_exact, half_low],
                near=[*range(1 + half_blocks, 1 + 2 * half_blocks), 2 + 2 * half_blocks],
                near_outs=(2,),
                room=8,
            )
        )
        order.ran(normed_back[-1][1])

    back_all_shape = ((rows, 3 * width), low)

    def attend_back():
        back_attn = order.after([member[1] for member in normed_back])
        made["attns"] = back_attn
        [made["all"]] = call(
            functools.partial(attend_back_kernel, widths, seqs),
            "attend_back",
            (seq_lengths, *back_attn, out_weight, queries, keys, values, totals),
            [back_all_shape],
            [((rows, model), low), outof, rows_width, rows_width, rows_width, totals_shape]
            + [rows_width, back_all_shape, ((rows, width), exact), ((rows, width), exact)],
            scalars=1,
            room=12,
        )
        order.ran(made["all"])

    def grad_attn():
        norm_sums = [member[2] for member in normed_back]
        up_sums = fed_back[0][half_blocks + 1] + fed_back[1][half_blocks + 1]
        small = jnp.concatenate(
            [
                jnp.zeros((1, model), jnp.float32),
                up_sums[0].reshape(-1, model),
                (norm_sums[0] + norm_sums[1])[:3],
                second_sums[:3],
            ]
        )
        small = jnp.pad(small, ((0, -small.shape[0] % 64), (0, 0)))
        made["small"] = small.shape[0]
        first_piece = ((model // 2, 2 * width), exact)
        second_rows = (width + model // 2 + small.shape[0]) // 2
        second_piece = ((second_rows, model), exact)
        [back_all] = order.after((made["all"],))
        pieces = call(
            grad_attn_kernel,
            "grad_attn",
            (first_bits("A"), tokens_in, back_all, context, *made["attns"], small),
            [first_piece, first_piece, second_piece, second_piece],
            [((rows, model), low), back_all_shape, rows_width, ((rows, model), low)]
            + [((model, 2 * width), exact), ((2 * second_rows, model), exact)],
            near=(6,),
            scalars=1,
            room=8,
        )
        order.ran(pieces[0])
        begin("A", [pieces[at] for at in (0, 2, 1, 3)])

    def input_part():
        [back_all] = order.after((made["all"],))
        made["parts"] = call(
            input_part_kernel,
            "input_part",
            (back_all, q_weight, k_weight, v_weight),
            [(block, exact)] * blocks,
            [back_all_shape, ((model, 3 * width), low), ((rows, model), exact)],
        )
        order.ran(made["parts"][-1])

    def grad_input():
        parts = made["parts"]
        others = order.after(swapped(parts))
        [result] = call(
            functools.partial(input_kernel, blocks),
            "grad_input",
            (*parts, *others, normed_back[0][0], normed_back[1][0]),
            [((rows, model), low)],
            [((rows, model), exact), ((rows, model), exact), ((rows, model), low)],
            near=range(blocks, 2 * blocks),
        )
        order.ran(result)
        made["input"] = result

    def finish(name, shapes, moves):
        operands = ()
        for chunk in (chunks[name + "0"], chunks[name + "1"]):
            operands += order.after(chunk.inputs())
        results = place_blocks(bits, operands, shapes, moves, "place")
        order.ran(results[0])
        return results

    def halves_at(name, rows, columns, target, row_offset, column, height):
        moves = []
        for at, same in enumerate((True, False)):
            first = at_bit(height, paths[name][0], same)
            moves.append(
                (
                    2 * int(name[1]) + at,
                    rows,
                    columns,
                    target,
                    lambda ref, first=first: row_offset + first(ref),
                    column,
                )
            )
        return moves

    half = hidden // 2
    quarter = half // 2
    columns_here = model // 2
    out_half, value_half = width // 2, model // 4
    tail_start = out_half + value_half
    square = (model, width)

    def place_down():
        [made["down"]] = finish(
            "D",
            ((hidden, model),),
            halves_at("D0", (0, quarter), (0, model), 0, 0, 0, quarter)
            + halves_at("D1", (0, quarter), (0, model), 0, half, 0, quarter),
        )

    def place_up():
        [made["up"]] = finish(
            "U",
            ((model, hidden),),
            halves_at("U0", (0, columns_here), (0, half), 0, 0, 0, columns_here)
            + halves_at("U1", (0, columns_here), (0, half), 0, 0, half, columns_here),
        )

    def place_attn():
        small_half = made["small"] // 2
        made["attn"] = finish(
            "A",
            (square, square, square, (width, model), (2 * small_half, model)),
            halves_at("A0", (0, columns_here), (0, width), 0, 0, 0, columns_here)
            + halves_at("A0", (0, columns_here), (width, 2 * width), 1, 0, 0, columns_here)
            + halves_at("A1", (out_half, tail_start), (0, width), 2, 0, 0, value_half)
            + halves_at(
                "A1", (out_half, tail_start), (width, 2 * width), 2, columns_here, 0, value_half
            )
            + halves_at("A1", (0, out_half), (0, model), 3, 0, 0, out_half)
            + halves_at("A1", (tail_start, tail_start + small_half), (0, model), 4, 0, 0, small_half),
        )

    steps = {
        "FB0": feed_back_first,
        "FB1": feed_back_last,
        "LN": first_norm_back,
        "AB": attend_back,
        "GA": grad_attn,
        "IP": input_part,
        "GI": grad_input,
        "PD": place_down,
        "PU": place_up,
        "PA": place_attn,
    }
    begin("D", down_pieces)
    for name in plan:
        if name in steps:
            steps[name]()
        else:
            run(name)
    grad_q, grad_k, grad_v, grad_out, tail = made["attn"]
    up_rows = hidden // model
    return (
        layer_out,
        made["input"],
        grad_q,
        grad_k,
        grad_v,
        tail[0, :width],
        tail[0, width:],
        grad_out,
        tail[up_rows + 1],
        tail[up_rows + 2],
        tail[up_rows + 3],
        made["up"],
        tail[1 : up_rows + 1].reshape(-1),
        made["down"],
        tail[up_rows + 4],
        tail[up_rows + 5],
        tail[up_rows + 6],
    )


def solution(mesh):
    placed = (
        P("dp", None),
        P("dp", None),
        P("dp", None),
        P(None, "tensor"),
        P(None, "tensor"),
        P(None, "tensor"),
        P("tensor"),
        P("tensor"),
        P("tensor", None),
        P(),
        P(),
        P(),
        P(None, "tensor"),
        P("tensor"),
        P("tensor", None),
        P(),
        P(),
        P(),
    )
    counts = (mesh.shape["dp"], mesh.shape["tensor"])

    def on_device(*args):
        return local(*counts, *args)

    return jax.shard_map(
        on_device,
        mesh=mesh,
        in_specs=placed,
        out_specs=(
            P("dp", None),
            P("dp", None),
            P(None, "tensor"),
            P(None, "tensor"),
            P(None, "tensor"),
            P("tensor"),
            P("tensor"),
            P("tensor", None),
            P(),
            P(),
            P(),
            P(None, "tensor"),
            P("tensor"),
            P("tensor", None),
            P(),
            P(),
            P(),
        ),
        check_vma=False,
    )
```

profile of v0, /device:TPU:0, one launch (start us, length us, event | category | flops | bytes accessed | tf_op | source)
XLA Modules:
  0.0 331.4 jit_solution(11289351470751930125)
XLA Ops:
  1.5 17.4 %attend.1 = (bf16[1024,384]{1,0:T(8,128)(2,1)}, bf16[1024,384]{1,0:T(8,128)(2,1)}, bf16[1024,384]{1,0:T(8,128)(2,1)}, bf16[1024,384]{1,0:T(8,128)(2,1)}, f32[12,...) custom-call(s32[1,4]{1,0:T(1,128)S(1)} %copy-done.9, ...), custom_call_target="tpu_custom_call" | custom-call | tf_op jit(solution)/shard_map/attend/pallas_call | solution.py:739
  22.7 6.6 %feed.2 = (f32[512,768]{1,0:T(8,128)}, bf16[512,768]{1,0:T(8,128)(2,1)}, bf16[512,1536]{1,0:T(8,128)(2,1)}, f32[256,768]{1,0:T(8,128)}, f32[256,768]{1,0:T(8,128)}) custom-call(bf16[1024,768]{1,0:T(8,128)(2,1)} %refs_1_.4, f32[256,768]{1,0:T(8,128)} %get-tuple-element.194.refs_1_, f32[256,768]{1,0:T(8,128)} %get-tuple-element.195.refs_2_, ...), custom_call_target="tpu_custom_call" | custom-call | tf_op jit(solution)/shard_map/feed/pallas_call | solution.py:739
  30.0 6.7 %feed.3 = (f32[512,768]{1,0:T(8,128)}, bf16[512,768]{1,0:T(8,128)(2,1)}, bf16[512,1536]{1,0:T(8,128)(2,1)}, f32[256,768]{1,0:T(8,128)}, f32[256,768]{1,0:T(8,128)}) custom-call(bf16[1024,768]{1,0:T(8,128)(2,1)} %refs_1_.4, f32[256,768]{1,0:T(8,128)} %get-tuple-element.197.refs_1_, f32[256,768]{1,0:T(8,128)} %get-tuple-element.198.refs_2_, ...), custom_call_target="tpu_custom_call" | custom-call | tf_op jit(solution)/shard_map/feed/pallas_call | solution.py:739
  37.3 6.0 %second_norm.2 = (bf16[1024,768]{1,0:T(8,128)(2,1)}, f32[512,768]{1,0:T(8,128)}, bf16[512,768]{1,0:T(8,128)(2,1)}, f32[8,768]{1,0:T(8,128)S(1)}) custom-call(f32[512,768]{1,0:T(8,128)} %get-tuple-element.200.refs_0_, f32[256,768]{1,0:T(8,128)} %get-tuple-element.201.refs_1_, f32[256,768]{1,0:T(8,128)} %get-tuple-element.202.refs_2_, ...), custom_call_target="tpu_custom_call" | custom-call | tf_op jit(solution)/shard_map/second_norm/pallas_call | solution.py:739
  43.4 9.6 %second_norm.3 = (bf16[1024,768]{1,0:T(8,128)(2,1)}, f32[512,768]{1,0:T(8,128)}, bf16[512,768]{1,0:T(8,128)(2,1)}, f32[8,768]{1,0:T(8,128)S(1)}, f32[384,768]{1,...) custom-call(s32[1,2]{1,0:T(1,128)S(1)} %add_bitcast_fusion.refs_0_, ...), custom_call_target="tpu_custom_call", output_to_operand_aliasing={{0}: (4, {})} | custom-call | tf_op jit(solution)/shard_map/second_norm/pallas_call | solution.py:739
  56.0 6.8 %feed_back.2 = (f32[256,768]{1,0:T(8,128)}, f32[256,768]{1,0:T(8,128)}, bf16[512,1536]{1,0:T(8,128)(2,1)}, f32[8,1536]{1,0:T(8,128)S(1)}) custom-call(bf16[512,768]{1,0:T(8,128)(2,1)} %get-tuple-element.210.refs_3_.refs_0_, bf16[512,768]{1,0:T(8,128)(2,1)} %get-tuple-element.211.refs_1_, bf16[768,1536]{1,0:T(8,128)(2,1)S(1)} %copy-done, f32[1536]{0:T(1024)S(1)} %copy-done.3, ...), custom_call_target="tpu_custom_call" | custom-call | tf_op jit(solution)/shard_map/feed_back/pallas_call | solution.py:739
  63.4 10.7 %feed_back.3 = (f32[256,768]{1,0:T(8,128)}, f32[256,768]{1,0:T(8,128)}, bf16[16,1536]{1,0:T(8,128)(2,1)}, f32[8,1536]{1,0:T(8,128)S(1)}, f32[384,768]{1,0:T(8,12...) custom-call(s32[1,2]{1,0:T(1,128)S(1)} %add_bitcast_fusion.refs_0_, ...), custom_call_target="tpu_custom_call" | custom-call | tf_op jit(solution)/shard_map/feed_back/pallas_call | solution.py:739
  74.7 5.6 %first_norm_back.2 = (f32[512,768]{1,0:T(8,128)}, bf16[512,768]{1,0:T(8,128)(2,1)}, f32[8,768]{1,0:T(8,128)S(1)}) custom-call(f32[512,768]{1,0:T(8,128)} %get-tuple-element.200.refs_0_, f32[256,768]{1,0:T(8,128)} %get-tuple-element.212.refs_1_, f32[256,768]{1,0:T(8,128)} %get-tuple-element.213.refs_2_, f32[256,768]{1,0:T(8,128)S(1)} %collective-permute-done.8.refs_3_, ...), custom_call_target="tpu_custom_call" | custom-call | tf_op jit(solution)/shard_map/first_norm_back/pallas_call | solution.py:739
  91.1 4.4 %first_norm_back.3 = (f32[512,768]{1,0:T(8,128)}, bf16[512,768]{1,0:T(8,128)(2,1)}, f32[8,768]{1,0:T(8,128)S(1)}) custom-call(f32[512,768]{1,0:T(8,128)} %get-tuple-element.205.refs_5_.refs_0_, f32[256,768]{1,0:T(8,128)} %get-tuple-element.222.refs_1_, f32[256,768]{1,0:T(8,128)} %get-tuple-element.223.refs_2_, ...), custom_call_target="tpu_custom_call" | custom-call | tf_op jit(solution)/shard_map/first_norm_back/pallas_call | solution.py:739
  95.6 20.3 %attend_back.1.refs_2_.refs_0_ = bf16[1024,1152]{1,0:T(8,128)(2,1)} custom-call(s32[1,4]{1,0:T(1,128)S(1)} %copy-done.10, bf16[512,768]{1,0:T(8,128)(2,1)} %get-tuple-element.235.refs_1_.refs_4_, bf16[512,768]{1,0:T(8,128)(2,1)} %get-tuple-element.236.refs_2_.refs_5_, bf16[384,768]{1,0:T(8,128)(2,1)} %refs_3_.6, ...), custom_call_target="tpu_custom_call" | custom-call | tf_op jit(solution)/shard_map/attend_back/pallas_call | solution.py:739
  115.9 6.0 %collective-permute-done.16 = f32[192,768]{1,0:T(8,128)} collective-permute-done((f32[192,768]{1,0:T(8,128)}, f32[192,768]{1,0:T(8,128)}, u32[]{:S(2)}, u32[]{:S(2)}) %collective-permute-start.16) | collective-permute-done | bytes 589856 | tf_op jit(solution)/shard_map/ppermute | solution.py:819
  131.0 8.1 %grad_attn.1 = (f32[384,768]{1,0:T(8,128)}, f32[384,768]{1,0:T(8,128)}, f32[416,768]{1,0:T(8,128)}, f32[416,768]{1,0:T(8,128)}) custom-call(s32[1,2]{1,0:T(1,128)S(1)} %add_bitcast_fusion.refs_0_, bf16[1024,768]{1,0:T(8,128)(2,1)} %refs_1_.4, bf16[1024,1152]{1,0:T(8,128)(2,1)} %attend_back.1.refs_2_.refs_0_, bf16[1024,384]{1,0:T(8,128)(2,1)} %get-tuple-element.252.refs_3_, ...), custom_call_target="tpu_custom_call" | custom-call | tf_op jit(solution)/shard_map/grad_attn/pallas_call | solution.py:739
  150.4 12.0 %collective-permute-done.21 = f32[192,768]{1,0:T(8,128)} collective-permute-done((f32[192,768]{1,0:T(8,128)}, f32[192,768]{1,0:T(8,128)}, u32[]{:S(2)}, u32[]{:S(2)}) %collective-permute-start.21) | collective-permute-done | bytes 589856 | tf_op jit(solution)/shard_map/ppermute | solution.py:819
  173.4 8.0 %collective-permute-done.26 = f32[96,768]{1,0:T(8,128)S(1)} collective-permute-done((f32[96,768]{1,0:T(8,128)S(1)}, f32[96,768]{1,0:T(8,128)S(1)}, u32[]{:S(2)}, u32[]{:S(2)}) %collective-permute-start.26) | collective-permute-done | bytes 294944 | tf_op jit(solution)/shard_map/ppermute | solution.py:819
  196.9 7.3 %collective-permute-done.34 = f32[192,768]{1,0:T(8,128)S(1)} collective-permute-done((f32[192,768]{1,0:T(8,128)S(1)}, f32[192,768]{1,0:T(8,128)S(1)}, u32[]{:S(2)}, u32[]{:S(2)}) %collective-permute-start.34) | collective-permute-done | bytes 589856 | tf_op jit(solution)/shard_map/ppermute | solution.py:819
  205.5 10.2 %collective-permute-done.33 = f32[96,768]{1,0:T(8,128)S(1)} collective-permute-done((f32[96,768]{1,0:T(8,128)S(1)}, f32[96,768]{1,0:T(8,128)S(1)}, u32[]{:S(2)}, u32[]{:S(2)}) %collective-permute-start.33) | collective-permute-done | bytes 294944 | tf_op jit(solution)/shard_map/ppermute | solution.py:819
  232.0 8.0 %collective-permute-done.36 = f32[104,768]{1,0:T(8,128)S(1)} collective-permute-done((f32[104,768]{1,0:T(8,128)S(1)}, f32[104,768]{1,0:T(8,128)S(1)}, u32[]{:S(2)}, u32[]{:S(2)}) %collective-permute-start.36) | collective-permute-done | bytes 319520 | tf_op jit(solution)/shard_map/ppermute | solution.py:819
  240.1 12.2 %collective-permute-done.41.refs_1_ = f32[192,768]{1,0:T(8,128)S(1)} collective-permute-done((f32[192,768]{1,0:T(8,128)S(1)}, f32[192,768]{1,0:T(8,128)S(1)}, u32[]{:S(2)}, u32[]{:S(2)}) %collective-permute-start.41) | collective-permute-done | bytes 589856 | tf_op jit(solution)/shard_map/ppermute | solution.py:819
  254.5 6.0 %collective-permute-done.40 = f32[104,768]{1,0:T(8,128)S(1)} collective-permute-done((f32[104,768]{1,0:T(8,128)S(1)}, f32[104,768]{1,0:T(8,128)S(1)}, u32[]{:S(2)}, u32[]{:S(2)}) %collective-permute-start.40) | collective-permute-done | bytes 319520 | tf_op jit(solution)/shard_map/ppermute | solution.py:819
  266.6 11.5 %collective-permute-done.47.refs_1_ = f32[96,768]{1,0:T(8,128)S(1)} collective-permute-done((f32[96,768]{1,0:T(8,128)S(1)}, f32[96,768]{1,0:T(8,128)S(1)}, u32[]{:S(2)}, u32[]{:S(2)}) %collective-permute-start.47) | collective-permute-done | bytes 294944 | tf_op jit(solution)/shard_map/ppermute | solution.py:819
  281.0 5.7 %input_part.1 = (f32[256,768]{1,0:T(8,128)}, f32[256,768]{1,0:T(8,128)}, f32[256,768]{1,0:T(8,128)}, f32[256,768]{1,0:T(8,128)}) custom-call(bf16[1024,1152]{1,0:T(8,128)(2,1)} %attend_back.1.refs_2_.refs_0_, bf16[768,384]{1,0:T(8,128)(2,1)} %refs_1_.5, bf16[768,384]{1,0:T(8,128)(2,1)} %refs_2_.5, bf16[768,384]{1,0:T(8,128)(2,1)} %refs_3_.7), custom_call_target="tpu_custom_call" | custom-call | tf_op jit(solution)/shard_map/input_part/pallas_call | solution.py:739
  289.6 7.7 %collective-permute-done.53.refs_1_ = f32[208,768]{1,0:T(8,128)S(1)} collective-permute-done((f32[208,768]{1,0:T(8,128)S(1)}, f32[208,768]{1,0:T(8,128)S(1)}, u32[]{:S(2)}, u32[]{:S(2)}) %collective-permute-start.53) | collective-permute-done | bytes 639008 | tf_op jit(solution)/shard_map/ppermute | solution.py:819
  304.5 4.3 %grad_input.1 = bf16[1024,768]{1,0:T(8,128)(2,1)} custom-call(f32[256,768]{1,0:T(8,128)} %get-tuple-element.344.refs_0_, f32[256,768]{1,0:T(8,128)} %get-tuple-element.345.refs_1_, f32[256,768]{1,0:T(8,128)} %get-tuple-element.346.refs_2_, f32[256,768]{1,0:T(8,128)} %get-tuple-element.347.refs_3_, f32[256,768]{1,0:T(8,128)S(1)} %collective-permute-done.48.refs_4_, ...), custom_call_target="tpu_custom_call" | custom-call | tf_op jit(solution)/shard_map/grad_input/pallas_call | solution.py:739
  308.9 17.5 %collective-permute-done.56.refs_1_ = f32[384,768]{1,0:T(8,128)S(1)} collective-permute-done((f32[384,768]{1,0:T(8,128)S(1)}, f32[384,768]{1,0:T(8,128)S(1)}, u32[]{:S(2)}, u32[]{:S(2)}) %collective-permute-start.56) | collective-permute-done | bytes 1179680 | tf_op jit(solution)/shard_map/ppermute | solution.py:819
  (223 shorter events, 111.0 us)
Async XLA Ops:
  52.9 28.6 %collective-permute-start.13 = (f32[384,768]{1,0:T(8,128)}, f32[384,768]{1,0:T(8,128)}, u32[]{:S(2)}, u32[]{:S(2)}) collective-permute-start(f32[384,768]{1,0:T(8,128)} %get-tuple-element.226), channel_id=1, source_target_pairs={{0,4},{2,6},{4,0},{6,2},{8,12},{10,14},{12,8},{14,10},{16,20},{18,... | collective-permute-start | bytes 3538952 | tf_op jit(solution)/shard_map/ppermute | solution.py:819
  53.1 31.5 %collective-permute-start.12 = (f32[384,768]{1,0:T(8,128)}, f32[384,768]{1,0:T(8,128)}, u32[]{:S(2)}, u32[]{:S(2)}) collective-permute-start(f32[384,768]{1,0:T(8,128)} %get-tuple-element.209), channel_id=1, source_target_pairs={{0,2},{2,0},{4,6},{6,4},{8,10},{10,8},{12,14},{14,12},{16,18},{18,... | collective-permute-start | bytes 3538952 | tf_op jit(solution)/shard_map/ppermute | solution.py:819
  74.6 52.1 %collective-permute-start.14 = (f32[384,768]{1,0:T(8,128)}, f32[384,768]{1,0:T(8,128)}, u32[]{:S(2)}, u32[]{:S(2)}) collective-permute-start(f32[384,768]{1,0:T(8,128)} %get-tuple-element.242), channel_id=1, source_target_pairs={{0,2},{2,0},{4,6},{6,4},{8,10},{10,8},{12,14},{14,12},{16,18},{18,... | collective-permute-start | bytes 3538952 | tf_op jit(solution)/shard_map/ppermute | solution.py:819
  81.6 57.7 %collective-permute-start.19 = (f32[384,768]{1,0:T(8,128)}, f32[384,768]{1,0:T(8,128)}, u32[]{:S(2)}, u32[]{:S(2)}) collective-permute-start(f32[384,768]{1,0:T(8,128)} %get-tuple-element.264), channel_id=1, source_target_pairs={{0,4},{2,6},{4,0},{6,2},{8,12},{10,14},{12,8},{14,10},{16,20},{18,... | collective-permute-start | bytes 3538952 | tf_op jit(solution)/shard_map/ppermute | solution.py:819
  87.1 34.8 %collective-permute-start.16 = (f32[192,768]{1,0:T(8,128)}, f32[192,768]{1,0:T(8,128)}, u32[]{:S(2)}, u32[]{:S(2)}) collective-permute-start(f32[192,768]{1,0:T(8,128)} %get-tuple-element.392), channel_id=1, source_target_pairs={{0,4},{2,6},{4,0},{6,2},{8,12},{10,14},{12,8},{14,10},{16,20},{18,... | collective-permute-start | bytes 1769480 | tf_op jit(solution)/shard_map/ppermute | solution.py:819
  88.5 37.3 %collective-permute-start.15 = (f32[192,768]{1,0:T(8,128)}, f32[192,768]{1,0:T(8,128)S(1)}, u32[]{:S(2)}, u32[]{:S(2)}) collective-permute-start(f32[192,768]{1,0:T(8,128)} %get-tuple-element.395), channel_id=1, source_target_pairs={{0,8},{2,10},{4,12},{6,14},{8,0},{10,2},{12,4},{14,6},{16,24},{18,... | collective-permute-start | bytes 1769480 | tf_op jit(solution)/shard_map/ppermute | solution.py:819
  142.6 21.7 %collective-permute-start.25 = (f32[96,768]{1,0:T(8,128)S(1)}, f32[96,768]{1,0:T(8,128)S(1)}, u32[]{:S(2)}, u32[]{:S(2)}) collective-permute-start(f32[96,768]{1,0:T(8,128)S(1)} %add_add_fusion.5), channel_id=1, source_target_pairs={{0,16},{2,18},{4,20},{6,22},{8,24},{10,26},{12,28},{14,30},{16,0},... | collective-permute-start | bytes 884744 | tf_op jit(solution)/shard_map/ppermute | solution.py:819
  144.8 19.8 %collective-permute-start.24 = (f32[96,768]{1,0:T(8,128)}, f32[96,768]{1,0:T(8,128)}, u32[]{:S(2)}, u32[]{:S(2)}) collective-permute-start(f32[96,768]{1,0:T(8,128)} %get-tuple-element.410), channel_id=1, source_target_pairs={{0,2},{2,0},{4,6},{6,4},{8,10},{10,8},{12,14},{14,12},{16,18},{18,... | collective-permute-start | bytes 884744 | tf_op jit(solution)/shard_map/ppermute | solution.py:819
  146.3 40.0 %collective-permute-start.18 = (f32[384,768]{1,0:T(8,128)}, f32[384,768]{1,0:T(8,128)}, u32[]{:S(2)}, u32[]{:S(2)}) collective-permute-start(f32[384,768]{1,0:T(8,128)} %get-tuple-element.262), channel_id=1, source_target_pairs={{0,2},{2,0},{4,6},{6,4},{8,10},{10,8},{12,14},{14,12},{16,18},{18,... | collective-permute-start | bytes 3538952 | tf_op jit(solution)/shard_map/ppermute | solution.py:819
  146.8 42.1 %collective-permute-start.17 = (f32[416,768]{1,0:T(8,128)}, f32[416,768]{1,0:T(8,128)}, u32[]{:S(2)}, u32[]{:S(2)}) collective-permute-start(f32[416,768]{1,0:T(8,128)} %get-tuple-element.260), channel_id=1, source_target_pairs={{0,4},{2,6},{4,0},{6,2},{8,12},{10,14},{12,8},{14,10},{16,20},{18,... | collective-permute-start | bytes 3833864 | tf_op jit(solution)/shard_map/ppermute | solution.py:819
  192.2 24.4 %collective-permute-start.32 = (f32[192,768]{1,0:T(8,128)S(1)}, f32[192,768]{1,0:T(8,128)S(1)}, u32[]{:S(2)}, u32[]{:S(2)}) collective-permute-start(f32[192,768]{1,0:T(8,128)S(1)} %join.12.refs_0_), channel_id=1, source_target_pairs={{0,4},{2,6},{4,0},{6,2},{8,12},{10,14},{12,8},{14,10},{16,20},{18,... | collective-permute-start | bytes 1769480 | tf_op jit(solution)/shard_map/ppermute | solution.py:819
  193.2 28.4 %collective-permute-start.28 = (f32[208,768]{1,0:T(8,128)}, f32[208,768]{1,0:T(8,128)}, u32[]{:S(2)}, u32[]{:S(2)}) collective-permute-start(f32[208,768]{1,0:T(8,128)} %get-tuple-element.379), channel_id=1, source_target_pairs={{0,2},{2,0},{4,6},{6,4},{8,10},{10,8},{12,14},{14,12},{16,18},{18,... | collective-permute-start | bytes 1916936 | tf_op jit(solution)/shard_map/ppermute | solution.py:819
  194.4 25.7 %collective-permute-start.31 = (f32[192,768]{1,0:T(8,128)S(1)}, f32[192,768]{1,0:T(8,128)S(1)}, u32[]{:S(2)}, u32[]{:S(2)}) collective-permute-start(f32[192,768]{1,0:T(8,128)S(1)} %join.13.refs_0_), channel_id=1, source_target_pairs={{0,8},{2,10},{4,12},{6,14},{8,0},{10,2},{12,4},{14,6},{16,24},{18,... | collective-permute-start | bytes 1769480 | tf_op jit(solution)/shard_map/ppermute | solution.py:819
  195.6 20.1 %collective-permute-start.33 = (f32[96,768]{1,0:T(8,128)S(1)}, f32[96,768]{1,0:T(8,128)S(1)}, u32[]{:S(2)}, u32[]{:S(2)}) collective-permute-start(f32[96,768]{1,0:T(8,128)S(1)} %add_add_fusion.2), channel_id=1, source_target_pairs={{0,16},{2,18},{4,20},{6,22},{8,24},{10,26},{12,28},{14,30},{16,0},... | collective-permute-start | bytes 884744 | tf_op jit(solution)/shard_map/ppermute | solution.py:819
  204.1 20.4 %collective-permute-start.39 = (f32[96,768]{1,0:T(8,128)S(1)}, f32[96,768]{1,0:T(8,128)S(1)}, u32[]{:S(2)}, u32[]{:S(2)}) collective-permute-start(f32[96,768]{1,0:T(8,128)S(1)} %add.262.refs_0_), channel_id=1, source_target_pairs={{0,8},{2,10},{4,12},{6,14},{8,0},{10,2},{12,4},{14,6},{16,24},{18,... | collective-permute-start | bytes 884744 | tf_op jit(solution)/shard_map/ppermute | solution.py:819
  220.1 41.3 %collective-permute-start.44 = (f32[384,768]{1,0:T(8,128)S(1)}, f32[384,768]{1,0:T(8,128)S(1)}, u32[]{:S(2)}, u32[]{:S(2)}) collective-permute-start(f32[384,768]{1,0:T(8,128)S(1)} %join.14.refs_0_), channel_id=1, source_target_pairs={{0,2},{2,0},{4,6},{6,4},{8,10},{10,8},{12,14},{14,12},{16,18},{18,... | collective-permute-start | bytes 3538952 | tf_op jit(solution)/shard_map/ppermute | solution.py:819
  221.7 39.9 %collective-permute-start.46 = (f32[384,768]{1,0:T(8,128)S(1)}, f32[384,768]{1,0:T(8,128)S(1)}, u32[]{:S(2)}, u32[]{:S(2)}) collective-permute-start(f32[384,768]{1,0:T(8,128)S(1)} %join.15.refs_2_), channel_id=1, source_target_pairs={{0,4},{2,6},{4,0},{6,2},{8,12},{10,14},{12,8},{14,10},{16,20},{18,... | collective-permute-start | bytes 3538952 | tf_op jit(solution)/shard_map/ppermute | solution.py:819
  225.8 34.8 %collective-permute-start.45 = (f32[192,768]{1,0:T(8,128)S(1)}, f32[192,768]{1,0:T(8,128)S(1)}, u32[]{:S(2)}, u32[]{:S(2)}) collective-permute-start(f32[192,768]{1,0:T(8,128)S(1)} %join.16.refs_0_), channel_id=1, source_target_pairs={{0,4},{2,6},{4,0},{6,2},{8,12},{10,14},{12,8},{14,10},{16,20},{18,... | collective-permute-start | bytes 1769480 | tf_op jit(solution)/shard_map/ppermute | solution.py:819
  229.8 22.6 %collective-permute-start.41 = (f32[192,768]{1,0:T(8,128)S(1)}, f32[192,768]{1,0:T(8,128)S(1)}, u32[]{:S(2)}, u32[]{:S(2)}) collective-permute-start(f32[192,768]{1,0:T(8,128)S(1)} %join.17.refs_0_), channel_id=1, source_target_pairs={{0,8},{2,10},{4,12},{6,14},{8,0},{10,2},{12,4},{14,6},{16,24},{18,... | collective-permute-start | bytes 1769480 | tf_op jit(solution)/shard_map/ppermute | solution.py:819
  240.1 20.5 %collective-permute-start.40 = (f32[104,768]{1,0:T(8,128)S(1)}, f32[104,768]{1,0:T(8,128)S(1)}, u32[]{:S(2)}, u32[]{:S(2)}) collective-permute-start(f32[104,768]{1,0:T(8,128)S(1)} %add_add_fusion), channel_id=1, source_target_pairs={{0,16},{2,18},{4,20},{6,22},{8,24},{10,26},{12,28},{14,30},{16,0},... | collective-permute-start | bytes 958472 | tf_op jit(solution)/shard_map/ppermute | solution.py:819
  260.5 26.3 %collective-permute-start.55 = (f32[384,768]{1,0:T(8,128)S(1)}, f32[384,768]{1,0:T(8,128)S(1)}, u32[]{:S(2)}, u32[]{:S(2)}) collective-permute-start(f32[384,768]{1,0:T(8,128)S(1)} %join.18.refs_2_), channel_id=1, source_target_pairs={{0,4},{2,6},{4,0},{6,2},{8,12},{10,14},{12,8},{14,10},{16,20},{18,... | collective-permute-start | bytes 3538952 | tf_op jit(solution)/shard_map/ppermute | solution.py:819
  261.4 25.4 %collective-permute-start.54 = (f32[384,768]{1,0:T(8,128)S(1)}, f32[384,768]{1,0:T(8,128)S(1)}, u32[]{:S(2)}, u32[]{:S(2)}) collective-permute-start(f32[384,768]{1,0:T(8,128)S(1)} %join.19.refs_0_), channel_id=1, source_target_pairs={{0,2},{2,0},{4,6},{6,4},{8,10},{10,8},{12,14},{14,12},{16,18},{18,... | collective-permute-start | bytes 3538952 | tf_op jit(solution)/shard_map/ppermute | solution.py:819
  298.2 28.1 %collective-permute-start.57 = (f32[416,768]{1,0:T(8,128)S(1)}, f32[416,768]{1,0:T(8,128)S(1)}, u32[]{:S(2)}, u32[]{:S(2)}) collective-permute-start(f32[416,768]{1,0:T(8,128)S(1)} %join.22.refs_2_), channel_id=1, source_target_pairs={{0,4},{2,6},{4,0},{6,2},{8,12},{10,14},{12,8},{14,10},{16,20},{18,... | collective-permute-start | bytes 3833864 | tf_op jit(solution)/shard_map/ppermute | solution.py:819
  299.4 26.9 %collective-permute-start.56 = (f32[384,768]{1,0:T(8,128)S(1)}, f32[384,768]{1,0:T(8,128)S(1)}, u32[]{:S(2)}, u32[]{:S(2)}) collective-permute-start(f32[384,768]{1,0:T(8,128)S(1)} %join.23.refs_0_), channel_id=1, source_target_pairs={{0,2},{2,0},{4,6},{6,4},{8,10},{10,8},{12,14},{14,12},{16,18},{18,... | collective-permute-start | bytes 3538952 | tf_op jit(solution)/shard_map/ppermute | solution.py:819
  (67 other events, 712.3 us)
where the time goes:
time: 338 us; the launch traced here: 331 us
  Pallas kernels  130 us (38%)
  waiting for transfers between devices  124 us (37%)
  starting transfers between devices  44.4 us (13%)
  other arithmetic  26.7 us (8%)
  local copies, waits for them, and re-layouts  4.66 us (1%)
    ppermute x42, waiting for transfers between devices, swap(): lax.ppermute(value, 'dp', [(i, i ^ 1 << bit) for i in range(self.count)])  117 us
    pallas_call x13, Pallas kernels, call(): pl.pallas_call(body, out_shape=tuple((struct(*out) if at in near_outs els...  112 us
    ppermute x42, starting transfers between devices, swap(): lax.ppermute(value, 'dp', [(i, i ^ 1 << bit) for i in range(self.count)])  40.3 us
    pallas_call x15, Pallas kernels, place_blocks(): pl.pallas_call(functools.partial(place_kernel, moves), out_shape=tuple((s...  17.5 us
    dynamic_slice x8, other arithmetic, half(): lax.dynamic_slice_in_dim(value, (mine if same else 1 - mine) * rows, rows...  13.8 us
    add x4, other arithmetic, advance(): functools.reduce(jnp.add, [ring.half(member, name, False) for member in i...  8.04 us
  transfers between devices with their start and end apart: 58, of which 22 were waited for; matrix products, arithmetic and copies ran while one was open for 8% of the time, Pallas kernels for 30%

commit v1 on v0

--- a/solution.py
+++ b/solution.py
@@ -913,10 +913,10 @@
 }
 
 plan = (
-    "D1", "D0", "FB0", "FB1", "LN", "D1", "D0", "LN", "AB", "U1", "D0", "U0", "D1", "U0", "GA",
-    "A1", "D0", "U1", "A0", "U0", "U1", "D0", "D1", "U0", "D1", "U1", "A0", "A1", "D0", "D1", "U0",
-    "A0", "U1", "D0", "D1", "A1", "U0", "U1", "A0", "A1", "U1", "A1", "U0", "PD", "A0", "A0", "A1",
-    "IP", "PU", "A1", "A0", "GI", "PA",
+    "D1", "D0", "FB0", "FB1", "LN", "U0", "D1", "D0", "LN", "AB", "U1", "D0", "U0", "D1", "GA",
+    "A1", "D0", "U1", "A0", "U0", "D0", "D1", "U1", "D1", "U0", "U1", "A0", "D0", "D1", "A1", "U0",
+    "A0", "U1", "D0", "A1", "D1", "U0", "U1", "A0", "A1", "U1", "A1", "U0", "PD", "A0", "IP", "A0",
+    "A1", "PU", "A0", "A1", "GI", "PA",
 )
 
 

time: 338 us -> 331 us (0.979)
  starting transfers between devices: 44.4 us -> 49 us
  other arithmetic: 26.7 us -> 22.2 us
    ppermute x42, starting transfers between devices: 40.3 us -> 45 us  [swap(): lax.ppermute(value, 'dp', [(i, i ^ 1 << bit) for i in range(self.count)])]
  transfers between devices with their start and end apart: 58 -> 58, of which waited for: 22 -> 24; matrix products, arithmetic and copies ran while one was open for 8% -> 7% of each run, Pallas kernels for 30% -> 30%
where the time goes in v1:
time: 331 us; the launch traced here: 324 us
  Pallas kernels  128 us (39%)
  waiting for transfers between devices  121 us (37%)
  starting transfers between devices  49 us (15%)
  other arithmetic  22.2 us (7%)
    ppermute x42, waiting for transfers between devices, swap(): lax.ppermute(value, 'dp', [(i, i ^ 1 << bit) for i in range(self.count)])  114 us
    pallas_call x13, Pallas kernels, call(): pl.pallas_call(body, out_shape=tuple((struct(*out) if at in near_outs els...  110 us
    ppermute x42, starting transfers between devices, swap(): lax.ppermute(value, 'dp', [(i, i ^ 1 << bit) for i in range(self.count)])  45 us
    pallas_call x15, Pallas kernels, place_blocks(): pl.pallas_call(functools.partial(place_kernel, moves), out_shape=tuple((s...  17.5 us
    dynamic_slice x8, other arithmetic, half(): lax.dynamic_slice_in_dim(value, (mine if same else 1 - mine) * rows, rows...  12.3 us
    ppermute x16, waiting for transfers between devices, swap_cores(): lax.ppermute(value, 'tensor', [(i, i ^ 1) for i in range(tensor_count)])  6.62 us
  transfers between devices with their start and end apart: 58, of which 24 were waited for; matrix products, arithmetic and copies ran while one was open for 7% of the time, Pallas kernels for 30%

profile of v1, /device:TPU:0, one launch (start us, length us, event | category | flops | bytes accessed | tf_op | source)
XLA Modules:
  0.0 324.3 jit_solution(16740197583148920054)
XLA Ops:
  1.5 16.6 %attend.1 = (bf16[1024,384]{1,0:T(8,128)(2,1)}, bf16[1024,384]{1,0:T(8,128)(2,1)}, bf16[1024,384]{1,0:T(8,128)(2,1)}, bf16[1024,384]{1,0:T(8,128)(2,1)}, f32[12,...) custom-call(s32[1,4]{1,0:T(1,128)S(1)} %copy-done.9, ...), custom_call_target="tpu_custom_call" | custom-call | tf_op jit(solution)/shard_map/attend/pallas_call | solution.py:739
  21.9 6.7 %feed.2 = (f32[512,768]{1,0:T(8,128)}, bf16[512,768]{1,0:T(8,128)(2,1)}, bf16[512,1536]{1,0:T(8,128)(2,1)}, f32[256,768]{1,0:T(8,128)}, f32[256,768]{1,0:T(8,128)}) custom-call(bf16[1024,768]{1,0:T(8,128)(2,1)} %refs_1_.4, f32[256,768]{1,0:T(8,128)} %get-tuple-element.194.refs_1_, f32[256,768]{1,0:T(8,128)} %get-tuple-element.195.refs_2_, ...), custom_call_target="tpu_custom_call" | custom-call | tf_op jit(solution)/shard_map/feed/pallas_call | solution.py:739
  29.1 6.6 %feed.3 = (f32[512,768]{1,0:T(8,128)}, bf16[512,768]{1,0:T(8,128)(2,1)}, bf16[512,1536]{1,0:T(8,128)(2,1)}, f32[256,768]{1,0:T(8,128)}, f32[256,768]{1,0:T(8,128)}) custom-call(bf16[1024,768]{1,0:T(8,128)(2,1)} %refs_1_.4, f32[256,768]{1,0:T(8,128)} %get-tuple-element.197.refs_1_, f32[256,768]{1,0:T(8,128)} %get-tuple-element.198.refs_2_, ...), custom_call_target="tpu_custom_call" | custom-call | tf_op jit(solution)/shard_map/feed/pallas_call | solution.py:739
  36.4 6.0 %second_norm.2 = (bf16[1024,768]{1,0:T(8,128)(2,1)}, f32[512,768]{1,0:T(8,128)}, bf16[512,768]{1,0:T(8,128)(2,1)}, f32[8,768]{1,0:T(8,128)S(1)}) custom-call(f32[512,768]{1,0:T(8,128)} %get-tuple-element.200.refs_0_, f32[256,768]{1,0:T(8,128)} %get-tuple-element.201.refs_1_, f32[256,768]{1,0:T(8,128)} %get-tuple-element.202.refs_2_, ...), custom_call_target="tpu_custom_call" | custom-call | tf_op jit(solution)/shard_map/second_norm/pallas_call | solution.py:739
  42.5 9.6 %second_norm.3 = (bf16[1024,768]{1,0:T(8,128)(2,1)}, f32[512,768]{1,0:T(8,128)}, bf16[512,768]{1,0:T(8,128)(2,1)}, f32[8,768]{1,0:T(8,128)S(1)}, f32[384,768]{1,...) custom-call(s32[1,2]{1,0:T(1,128)S(1)} %add_bitcast_fusion.refs_0_, ...), custom_call_target="tpu_custom_call", output_to_operand_aliasing={{0}: (4, {})} | custom-call | tf_op jit(solution)/shard_map/second_norm/pallas_call | solution.py:739
  56.0 6.8 %feed_back.2 = (f32[256,768]{1,0:T(8,128)}, f32[256,768]{1,0:T(8,128)}, bf16[512,1536]{1,0:T(8,128)(2,1)}, f32[8,1536]{1,0:T(8,128)S(1)}) custom-call(bf16[512,768]{1,0:T(8,128)(2,1)} %get-tuple-element.210.refs_3_.refs_0_, bf16[512,768]{1,0:T(8,128)(2,1)} %get-tuple-element.211.refs_1_, bf16[768,1536]{1,0:T(8,128)(2,1)S(1)} %copy-done, f32[1536]{0:T(1024)S(1)} %copy-done.3, ...), custom_call_target="tpu_custom_call" | custom-call | tf_op jit(solution)/shard_map/feed_back/pallas_call | solution.py:739
  63.3 10.6 %feed_back.3 = (f32[256,768]{1,0:T(8,128)}, f32[256,768]{1,0:T(8,128)}, bf16[16,1536]{1,0:T(8,128)(2,1)}, f32[8,1536]{1,0:T(8,128)S(1)}, f32[384,768]{1,0:T(8,12...) custom-call(s32[1,2]{1,0:T(1,128)S(1)} %add_bitcast_fusion.refs_0_, ...), custom_call_target="tpu_custom_call" | custom-call | tf_op jit(solution)/shard_map/feed_back/pallas_call | solution.py:739
  74.6 5.7 %first_norm_back.2 = (f32[512,768]{1,0:T(8,128)}, bf16[512,768]{1,0:T(8,128)(2,1)}, f32[8,768]{1,0:T(8,128)S(1)}) custom-call(f32[512,768]{1,0:T(8,128)} %get-tuple-element.200.refs_0_, f32[256,768]{1,0:T(8,128)} %get-tuple-element.212.refs_1_, f32[256,768]{1,0:T(8,128)} %get-tuple-element.213.refs_2_, f32[256,768]{1,0:T(8,128)S(1)} %collective-permute-done.8.refs_3_, ...), custom_call_target="tpu_custom_call" | custom-call | tf_op jit(solution)/shard_map/first_norm_back/pallas_call | solution.py:739
  91.1 4.4 %first_norm_back.3 = (f32[512,768]{1,0:T(8,128)}, bf16[512,768]{1,0:T(8,128)(2,1)}, f32[8,768]{1,0:T(8,128)S(1)}) custom-call(f32[512,768]{1,0:T(8,128)} %get-tuple-element.205.refs_5_.refs_0_, f32[256,768]{1,0:T(8,128)} %get-tuple-element.222.refs_1_, f32[256,768]{1,0:T(8,128)} %get-tuple-element.223.refs_2_, ...), custom_call_target="tpu_custom_call" | custom-call | tf_op jit(solution)/shard_map/first_norm_back/pallas_call | solution.py:739
  95.6 19.1 %attend_back.1.refs_2_.refs_0_ = bf16[1024,1152]{1,0:T(8,128)(2,1)} custom-call(s32[1,4]{1,0:T(1,128)S(1)} %copy-done.10, bf16[512,768]{1,0:T(8,128)(2,1)} %get-tuple-element.235.refs_1_.refs_4_, bf16[512,768]{1,0:T(8,128)(2,1)} %get-tuple-element.236.refs_2_.refs_5_, bf16[384,768]{1,0:T(8,128)(2,1)} %refs_3_.6, ...), custom_call_target="tpu_custom_call" | custom-call | tf_op jit(solution)/shard_map/attend_back/pallas_call | solution.py:739
  114.7 6.8 %collective-permute-done.16 = f32[192,768]{1,0:T(8,128)} collective-permute-done((f32[192,768]{1,0:T(8,128)}, f32[192,768]{1,0:T(8,128)}, u32[]{:S(2)}, u32[]{:S(2)}) %collective-permute-start.16) | collective-permute-done | bytes 589856 | tf_op jit(solution)/shard_map/ppermute | solution.py:819
  130.4 8.1 %grad_attn.1 = (f32[384,768]{1,0:T(8,128)}, f32[384,768]{1,0:T(8,128)}, f32[416,768]{1,0:T(8,128)}, f32[416,768]{1,0:T(8,128)}) custom-call(s32[1,2]{1,0:T(1,128)S(1)} %add_bitcast_fusion.refs_0_, bf16[1024,768]{1,0:T(8,128)(2,1)} %refs_1_.4, bf16[1024,1152]{1,0:T(8,128)(2,1)} %attend_back.1.refs_2_.refs_0_, bf16[1024,384]{1,0:T(8,128)(2,1)} %get-tuple-element.252.refs_3_, ...), custom_call_target="tpu_custom_call" | custom-call | tf_op jit(solution)/shard_map/grad_attn/pallas_call | solution.py:739
  144.9 7.4 %collective-permute-done.22 = f32[96,768]{1,0:T(8,128)S(1)} collective-permute-done((f32[96,768]{1,0:T(8,128)S(1)}, f32[96,768]{1,0:T(8,128)S(1)}, u32[]{:S(2)}, u32[]{:S(2)}) %collective-permute-start.22) | collective-permute-done | bytes 294944 | tf_op jit(solution)/shard_map/ppermute | solution.py:819
  154.5 14.8 %collective-permute-done.20 = f32[192,768]{1,0:T(8,128)} collective-permute-done((f32[192,768]{1,0:T(8,128)S(1)}, f32[192,768]{1,0:T(8,128)}, u32[]{:S(2)}, u32[]{:S(2)}) %collective-permute-start.20) | collective-permute-done | bytes 589856 | tf_op jit(solution)/shard_map/ppermute | solution.py:819
  193.2 4.5 %collective-permute-done.27 = f32[192,768]{1,0:T(8,128)S(1)} collective-permute-done((f32[192,768]{1,0:T(8,128)S(1)}, f32[192,768]{1,0:T(8,128)S(1)}, u32[]{:S(2)}, u32[]{:S(2)}) %collective-permute-start.27) | collective-permute-done | bytes 589856 | tf_op jit(solution)/shard_map/ppermute | solution.py:819
  198.7 10.8 %collective-permute-done.33 = f32[96,768]{1,0:T(8,128)S(1)} collective-permute-done((f32[96,768]{1,0:T(8,128)S(1)}, f32[96,768]{1,0:T(8,128)S(1)}, u32[]{:S(2)}, u32[]{:S(2)}) %collective-permute-start.33) | collective-permute-done | bytes 294944 | tf_op jit(solution)/shard_map/ppermute | solution.py:819
  225.6 9.2 %collective-permute-done.42 = f32[104,768]{1,0:T(8,128)S(1)} collective-permute-done((f32[104,768]{1,0:T(8,128)S(1)}, f32[104,768]{1,0:T(8,128)S(1)}, u32[]{:S(2)}, u32[]{:S(2)}) %collective-permute-start.42) | collective-permute-done | bytes 319520 | tf_op jit(solution)/shard_map/ppermute | solution.py:819
  235.0 11.1 %collective-permute-done.44.refs_1_ = f32[192,768]{1,0:T(8,128)S(1)} collective-permute-done((f32[192,768]{1,0:T(8,128)S(1)}, f32[192,768]{1,0:T(8,128)S(1)}, u32[]{:S(2)}, u32[]{:S(2)}) %collective-permute-start.44) | collective-permute-done | bytes 589856 | tf_op jit(solution)/shard_map/ppermute | solution.py:819
  246.9 7.2 %collective-permute-done.43 = f32[104,768]{1,0:T(8,128)S(1)} collective-permute-done((f32[104,768]{1,0:T(8,128)S(1)}, f32[104,768]{1,0:T(8,128)S(1)}, u32[]{:S(2)}, u32[]{:S(2)}) %collective-permute-start.43) | collective-permute-done | bytes 319520 | tf_op jit(solution)/shard_map/ppermute | solution.py:819
  260.1 5.7 %input_part.1 = (f32[256,768]{1,0:T(8,128)}, f32[256,768]{1,0:T(8,128)}, f32[256,768]{1,0:T(8,128)}, f32[256,768]{1,0:T(8,128)}) custom-call(bf16[1024,1152]{1,0:T(8,128)(2,1)} %attend_back.1.refs_2_.refs_0_, bf16[768,384]{1,0:T(8,128)(2,1)} %refs_1_.5, bf16[768,384]{1,0:T(8,128)(2,1)} %refs_2_.5, bf16[768,384]{1,0:T(8,128)(2,1)} %refs_3_.7), custom_call_target="tpu_custom_call" | custom-call | tf_op jit(solution)/shard_map/input_part/pallas_call | solution.py:739
  265.7 5.4 %collective-permute-done.51.refs_1_ = f32[96,768]{1,0:T(8,128)S(1)} collective-permute-done((f32[96,768]{1,0:T(8,128)S(1)}, f32[96,768]{1,0:T(8,128)S(1)}, u32[]{:S(2)}, u32[]{:S(2)}) %collective-permute-start.51) | collective-permute-done | bytes 294944 | tf_op jit(solution)/shard_map/ppermute | solution.py:819
  274.7 4.9 %collective-permute-done.54.refs_1_ = f32[384,768]{1,0:T(8,128)S(1)} collective-permute-done((f32[384,768]{1,0:T(8,128)S(1)}, f32[384,768]{1,0:T(8,128)S(1)}, u32[]{:S(2)}, u32[]{:S(2)}) %collective-permute-start.54) | collective-permute-done | bytes 1179680 | tf_op jit(solution)/shard_map/ppermute | solution.py:819
  282.4 5.6 %collective-permute-done.53.refs_1_ = f32[192,768]{1,0:T(8,128)S(1)} collective-permute-done((f32[192,768]{1,0:T(8,128)S(1)}, f32[192,768]{1,0:T(8,128)S(1)}, u32[]{:S(2)}, u32[]{:S(2)}) %collective-permute-start.53) | collective-permute-done | bytes 589856 | tf_op jit(solution)/shard_map/ppermute | solution.py:819
  301.2 17.3 %collective-permute-done.56.refs_1_ = f32[384,768]{1,0:T(8,128)S(1)} collective-permute-done((f32[384,768]{1,0:T(8,128)S(1)}, f32[384,768]{1,0:T(8,128)S(1)}, u32[]{:S(2)}, u32[]{:S(2)}) %collective-permute-start.56) | collective-permute-done | bytes 1179680 | tf_op jit(solution)/shard_map/ppermute | solution.py:819
  (219 shorter events, 111.7 us)
Async XLA Ops:
  52.1 28.6 %collective-permute-start.13 = (f32[384,768]{1,0:T(8,128)}, f32[384,768]{1,0:T(8,128)}, u32[]{:S(2)}, u32[]{:S(2)}) collective-permute-start(f32[384,768]{1,0:T(8,128)} %get-tuple-element.226), channel_id=1, source_target_pairs={{0,4},{2,6},{4,0},{6,2},{8,12},{10,14},{12,8},{14,10},{16,20},{18,... | collective-permute-start | bytes 3538952 | tf_op jit(solution)/shard_map/ppermute | solution.py:819
  53.1 31.5 %collective-permute-start.12 = (f32[384,768]{1,0:T(8,128)}, f32[384,768]{1,0:T(8,128)}, u32[]{:S(2)}, u32[]{:S(2)}) collective-permute-start(f32[384,768]{1,0:T(8,128)} %get-tuple-element.209), channel_id=1, source_target_pairs={{0,2},{2,0},{4,6},{6,4},{8,10},{10,8},{12,14},{14,12},{16,18},{18,... | collective-permute-start | bytes 3538952 | tf_op jit(solution)/shard_map/ppermute | solution.py:819
  74.6 51.3 %collective-permute-start.15 = (f32[384,768]{1,0:T(8,128)}, f32[384,768]{1,0:T(8,128)}, u32[]{:S(2)}, u32[]{:S(2)}) collective-permute-start(f32[384,768]{1,0:T(8,128)} %get-tuple-element.242), channel_id=1, source_target_pairs={{0,2},{2,0},{4,6},{6,4},{8,10},{10,8},{12,14},{14,12},{16,18},{18,... | collective-permute-start | bytes 3538952 | tf_op jit(solution)/shard_map/ppermute | solution.py:819
  80.7 59.1 %collective-permute-start.18 = (f32[384,768]{1,0:T(8,128)}, f32[384,768]{1,0:T(8,128)}, u32[]{:S(2)}, u32[]{:S(2)}) collective-permute-start(f32[384,768]{1,0:T(8,128)} %get-tuple-element.262), channel_id=1, source_target_pairs={{0,4},{2,6},{4,0},{6,2},{8,12},{10,14},{12,8},{14,10},{16,20},{18,... | collective-permute-start | bytes 3538952 | tf_op jit(solution)/shard_map/ppermute | solution.py:819
  87.1 34.4 %collective-permute-start.16 = (f32[192,768]{1,0:T(8,128)}, f32[192,768]{1,0:T(8,128)}, u32[]{:S(2)}, u32[]{:S(2)}) collective-permute-start(f32[192,768]{1,0:T(8,128)} %get-tuple-element.392), channel_id=1, source_target_pairs={{0,4},{2,6},{4,0},{6,2},{8,12},{10,14},{12,8},{14,10},{16,20},{18,... | collective-permute-start | bytes 1769480 | tf_op jit(solution)/shard_map/ppermute | solution.py:819
  87.6 41.1 %collective-permute-start.14 = (f32[192,768]{1,0:T(8,128)}, f32[192,768]{1,0:T(8,128)S(1)}, u32[]{:S(2)}, u32[]{:S(2)}) collective-permute-start(f32[192,768]{1,0:T(8,128)} %get-tuple-element.395), channel_id=1, source_target_pairs={{0,8},{2,10},{4,12},{6,14},{8,0},{10,2},{12,4},{14,6},{16,24},{18,... | collective-permute-start | bytes 1769480 | tf_op jit(solution)/shard_map/ppermute | solution.py:819
  128.9 23.5 %collective-permute-start.21 = (f32[96,768]{1,0:T(8,128)S(1)}, f32[96,768]{1,0:T(8,128)S(1)}, u32[]{:S(2)}, u32[]{:S(2)}) collective-permute-start(f32[96,768]{1,0:T(8,128)S(1)} %get-tuple-element.414), channel_id=1, source_target_pairs={{0,2},{2,0},{4,6},{6,4},{8,10},{10,8},{12,14},{14,12},{16,18},{18,... | collective-permute-start | bytes 884744 | tf_op jit(solution)/shard_map/ppermute | solution.py:819
  141.3 28.0 %collective-permute-start.20 = (f32[192,768]{1,0:T(8,128)S(1)}, f32[192,768]{1,0:T(8,128)}, u32[]{:S(2)}, u32[]{:S(2)}) collective-permute-start(f32[192,768]{1,0:T(8,128)S(1)} %get-tuple-element.388), channel_id=1, source_target_pairs={{0,8},{2,10},{4,12},{6,14},{8,0},{10,2},{12,4},{14,6},{16,24},{18,... | collective-permute-start | bytes 1769480 | tf_op jit(solution)/shard_map/ppermute | solution.py:819
  141.5 39.5 %collective-permute-start.17 = (f32[384,768]{1,0:T(8,128)}, f32[384,768]{1,0:T(8,128)}, u32[]{:S(2)}, u32[]{:S(2)}) collective-permute-start(f32[384,768]{1,0:T(8,128)} %get-tuple-element.260), channel_id=1, source_target_pairs={{0,2},{2,0},{4,6},{6,4},{8,10},{10,8},{12,14},{14,12},{16,18},{18,... | collective-permute-start | bytes 3538952 | tf_op jit(solution)/shard_map/ppermute | solution.py:819
  143.5 42.4 %collective-permute-start.29 = (f32[416,768]{1,0:T(8,128)}, f32[416,768]{1,0:T(8,128)}, u32[]{:S(2)}, u32[]{:S(2)}) collective-permute-start(f32[416,768]{1,0:T(8,128)} %get-tuple-element.294), channel_id=1, source_target_pairs={{0,4},{2,6},{4,0},{6,2},{8,12},{10,14},{12,8},{14,10},{16,20},{18,... | collective-permute-start | bytes 3833864 | tf_op jit(solution)/shard_map/ppermute | solution.py:819
  152.5 20.6 %collective-permute-start.26 = (f32[96,768]{1,0:T(8,128)S(1)}, f32[96,768]{1,0:T(8,128)S(1)}, u32[]{:S(2)}, u32[]{:S(2)}) collective-permute-start(f32[96,768]{1,0:T(8,128)S(1)} %add_add_fusion.4), channel_id=1, source_target_pairs={{0,16},{2,18},{4,20},{6,22},{8,24},{10,26},{12,28},{14,30},{16,0},... | collective-permute-start | bytes 884744 | tf_op jit(solution)/shard_map/ppermute | solution.py:819
  152.5 23.0 %collective-permute-start.25 = (f32[96,768]{1,0:T(8,128)S(1)}, f32[96,768]{1,0:T(8,128)}, u32[]{:S(2)}, u32[]{:S(2)}) collective-permute-start(f32[96,768]{1,0:T(8,128)S(1)} %get-tuple-element.406), channel_id=1, source_target_pairs={{0,8},{2,10},{4,12},{6,14},{8,0},{10,2},{12,4},{14,6},{16,24},{18,... | collective-permute-start | bytes 884744 | tf_op jit(solution)/shard_map/ppermute | solution.py:819
  185.1 26.2 %collective-permute-start.38 = (f32[192,768]{1,0:T(8,128)S(1)}, f32[192,768]{1,0:T(8,128)S(1)}, u32[]{:S(2)}, u32[]{:S(2)}) collective-permute-start(f32[192,768]{1,0:T(8,128)S(1)} %join.12.refs_0_), channel_id=1, source_target_pairs={{0,4},{2,6},{4,0},{6,2},{8,12},{10,14},{12,8},{14,10},{16,20},{18,... | collective-permute-start | bytes 1769480 | tf_op jit(solution)/shard_map/ppermute | solution.py:819
  188.5 26.5 %collective-permute-start.37 = (f32[208,768]{1,0:T(8,128)}, f32[208,768]{1,0:T(8,128)}, u32[]{:S(2)}, u32[]{:S(2)}) collective-permute-start(f32[208,768]{1,0:T(8,128)} %get-tuple-element.380), channel_id=1, source_target_pairs={{0,2},{2,0},{4,6},{6,4},{8,10},{10,8},{12,14},{14,12},{16,18},{18,... | collective-permute-start | bytes 1916936 | tf_op jit(solution)/shard_map/ppermute | solution.py:819
  190.3 26.4 %collective-permute-start.36 = (f32[192,768]{1,0:T(8,128)S(1)}, f32[192,768]{1,0:T(8,128)S(1)}, u32[]{:S(2)}, u32[]{:S(2)}) collective-permute-start(f32[192,768]{1,0:T(8,128)S(1)} %join.13.refs_0_), channel_id=1, source_target_pairs={{0,8},{2,10},{4,12},{6,14},{8,0},{10,2},{12,4},{14,6},{16,24},{18,... | collective-permute-start | bytes 1769480 | tf_op jit(solution)/shard_map/ppermute | solution.py:819
  197.7 23.2 %collective-permute-start.35 = (f32[96,768]{1,0:T(8,128)S(1)}, f32[96,768]{1,0:T(8,128)S(1)}, u32[]{:S(2)}, u32[]{:S(2)}) collective-permute-start(f32[96,768]{1,0:T(8,128)S(1)} %add.261.refs_0_), channel_id=1, source_target_pairs={{0,8},{2,10},{4,12},{6,14},{8,0},{10,2},{12,4},{14,6},{16,24},{18,... | collective-permute-start | bytes 884744 | tf_op jit(solution)/shard_map/ppermute | solution.py:819
  215.1 40.1 %collective-permute-start.40 = (f32[384,768]{1,0:T(8,128)S(1)}, f32[384,768]{1,0:T(8,128)S(1)}, u32[]{:S(2)}, u32[]{:S(2)}) collective-permute-start(f32[384,768]{1,0:T(8,128)S(1)} %join.14.refs_0_), channel_id=1, source_target_pairs={{0,2},{2,0},{4,6},{6,4},{8,10},{10,8},{12,14},{14,12},{16,18},{18,... | collective-permute-start | bytes 3538952 | tf_op jit(solution)/shard_map/ppermute | solution.py:819
  217.6 37.6 %collective-permute-start.45 = (f32[384,768]{1,0:T(8,128)S(1)}, f32[384,768]{1,0:T(8,128)S(1)}, u32[]{:S(2)}, u32[]{:S(2)}) collective-permute-start(f32[384,768]{1,0:T(8,128)S(1)} %join.15.refs_2_), channel_id=1, source_target_pairs={{0,4},{2,6},{4,0},{6,2},{8,12},{10,14},{12,8},{14,10},{16,20},{18,... | collective-permute-start | bytes 3538952 | tf_op jit(solution)/shard_map/ppermute | solution.py:819
  221.6 32.5 %collective-permute-start.41 = (f32[192,768]{1,0:T(8,128)S(1)}, f32[192,768]{1,0:T(8,128)S(1)}, u32[]{:S(2)}, u32[]{:S(2)}) collective-permute-start(f32[192,768]{1,0:T(8,128)S(1)} %join.16.refs_0_), channel_id=1, source_target_pairs={{0,4},{2,6},{4,0},{6,2},{8,12},{10,14},{12,8},{14,10},{16,20},{18,... | collective-permute-start | bytes 1769480 | tf_op jit(solution)/shard_map/ppermute | solution.py:819
  222.5 23.6 %collective-permute-start.44 = (f32[192,768]{1,0:T(8,128)S(1)}, f32[192,768]{1,0:T(8,128)S(1)}, u32[]{:S(2)}, u32[]{:S(2)}) collective-permute-start(f32[192,768]{1,0:T(8,128)S(1)} %join.17.refs_0_), channel_id=1, source_target_pairs={{0,8},{2,10},{4,12},{6,14},{8,0},{10,2},{12,4},{14,6},{16,24},{18,... | collective-permute-start | bytes 1769480 | tf_op jit(solution)/shard_map/ppermute | solution.py:819
  254.1 20.7 %collective-permute-start.55 = (f32[384,768]{1,0:T(8,128)S(1)}, f32[384,768]{1,0:T(8,128)S(1)}, u32[]{:S(2)}, u32[]{:S(2)}) collective-permute-start(f32[384,768]{1,0:T(8,128)S(1)} %join.18.refs_2_), channel_id=1, source_target_pairs={{0,4},{2,6},{4,0},{6,2},{8,12},{10,14},{12,8},{14,10},{16,20},{18,... | collective-permute-start | bytes 3538952 | tf_op jit(solution)/shard_map/ppermute | solution.py:819
  254.9 24.7 %collective-permute-start.54 = (f32[384,768]{1,0:T(8,128)S(1)}, f32[384,768]{1,0:T(8,128)S(1)}, u32[]{:S(2)}, u32[]{:S(2)}) collective-permute-start(f32[384,768]{1,0:T(8,128)S(1)} %join.19.refs_0_), channel_id=1, source_target_pairs={{0,2},{2,0},{4,6},{6,4},{8,10},{10,8},{12,14},{14,12},{16,18},{18,... | collective-permute-start | bytes 3538952 | tf_op jit(solution)/shard_map/ppermute | solution.py:819
  291.6 27.6 %collective-permute-start.57 = (f32[416,768]{1,0:T(8,128)S(1)}, f32[416,768]{1,0:T(8,128)S(1)}, u32[]{:S(2)}, u32[]{:S(2)}) collective-permute-start(f32[416,768]{1,0:T(8,128)S(1)} %join.23.refs_2_), channel_id=1, source_target_pairs={{0,4},{2,6},{4,0},{6,2},{8,12},{10,14},{12,8},{14,10},{16,20},{18,... | collective-permute-start | bytes 3833864 | tf_op jit(solution)/shard_map/ppermute | solution.py:819
  292.0 26.6 %collective-permute-start.56 = (f32[384,768]{1,0:T(8,128)S(1)}, f32[384,768]{1,0:T(8,128)S(1)}, u32[]{:S(2)}, u32[]{:S(2)}) collective-permute-start(f32[384,768]{1,0:T(8,128)S(1)} %join.22.refs_0_), channel_id=1, source_target_pairs={{0,2},{2,0},{4,6},{6,4},{8,10},{10,8},{12,14},{14,12},{16,18},{18,... | collective-permute-start | bytes 3538952 | tf_op jit(solution)/shard_map/ppermute | solution.py:819
  (65 other events, 666.7 us)
